TPU v7x, 32 devices: a whole 2x2x4 slice. The times are simulated.
32 devices in a mesh: groups: 2 (over y), vox: 4 (over z), chan: 2 (over x), frm: 2 (over core).
Axes of the slice: x: 2, y: 2, z: 4, core: 2. Of those that a mesh axis runs over, the one named last changes fastest.
Arguments:
- echo_data: bfloat16 [8, 2, 1024, 2, 512], P(('groups', 'vox'), 'chan', None, None, 'frm'), parts along dimension 0, may hold values from -36 to 36
- tile_weights: bfloat16 [4, 2, 64, 128, 128], P('vox', 'chan'), may hold values from -0.0625 to 0.0625
- tile_target: int32 [4, 2, 64], P('vox', 'chan'), may hold values from 0 to 1
- tile_offset: int32 [4, 2, 64], P('vox', 'chan'), may hold values from 0 to 896
- tile_count: int32 [4, 2], P('vox', 'chan'), may hold values from 8 to 64, as said below
- grid_map: int32 [4, 256], P('vox'), may hold values from 0 to 255, each once within a row
- psf_kernel: float32 [5, 5], replicated, may hold values from -1.25 to 1.25
Outputs:
- psf_image: float32 [64, 32, 512], P(('groups', 'vox'), 'chan', 'frm'), parts along dimension 0
There are 2 independent parts, one for each index of `groups`. A program takes and returns all parts, laid end to end along the dimension named above; an argument that names none is the same for every part. Nothing has to cross between parts.
Inputs may be any that keep to these rules, and one draw needn't show every extreme that they name: `tile_count`: in each voxel block exactly one channel group uses all 64 slots; the others use far fewer. `grid_map`: each block's row is a permutation of 0 to 255.
All inputs are finite; a program needn't handle non-finite values.
Results may differ from a plain program's by a relative error of at most 0.014.
Values may be sent and summed in bfloat16 or wider, within the bound.
A program may use at most 64 MiB of HBM per device.

v0:
```python
import functools

import jax
import jax.numpy as jnp
from jax import lax
from jax.experimental import pallas as pl
from jax.experimental.pallas import tpu as pltpu
from jax.sharding import PartitionSpec as P

MESH = pl.DeviceIdType.MESH
PIECES = 4
GROUP = 8

TBATCH = 8
LAT_DEV = 8


POLY_COEFFS = (1.0, -0.6, 0.15, -0.03)


def with_halo(shard, sides, width):
    for axis, dim in sides:
        devices, length = (lax.axis_size(axis), shard.shape[dim])
        up = [(i, (i + 1) % devices) for i in range(devices - 1)]
        down = [(j, i) for i, j in up]
        last = lax.slice_in_dim(shard, length - width, length, axis=dim)
        leading = lax.slice_in_dim(shard, 0, width, axis=dim)
        before = lax.ppermute(last, axis, up)
        after = lax.ppermute(leading, axis, down)
        shard = jnp.concatenate([before, shard, after], axis=dim)
    return shard


def complex_times(left_real, left_imag, right_real, right_imag):
    level = lax.Precision.HIGH
    real_part = jnp.dot(
        left_real, right_real, precision=level, preferred_element_type=jnp.float32
    ) - jnp.dot(left_imag, right_imag, precision=level, preferred_element_type=jnp.float32)
    imag_part = jnp.dot(
        left_real, right_imag, precision=level, preferred_element_type=jnp.float32
    ) + jnp.dot(left_imag, right_real, precision=level, preferred_element_type=jnp.float32)
    return (real_part, imag_part)


def tile_pass(flat_echo, weights, tile_goal, tile_start, live_total, tiles_out):
    tile_size = weights.shape[-1]
    col_count = flat_echo.shape[-1]
    slot_count = weights.shape[0]
    lane_ids = jnp.arange(TBATCH, dtype=jnp.int32)
    target_ids = jnp.arange(tiles_out, dtype=jnp.int32)
    zero_index = jnp.zeros((), jnp.int32)

    def cut_rows(offset_id):
        return lax.dynamic_slice(flat_echo, (offset_id, zero_index), (tile_size, col_count))

    def one_turn(turn_index, totals):
        where_at = turn_index * TBATCH + lane_ids
        live_lane = where_at < live_total
        chosen = jnp.minimum(where_at, slot_count - 1)
        picked = weights[chosen]
        samples = jax.vmap(cut_rows)(tile_start[chosen])
        product = jnp.einsum("krs,ksc->krc", picked, samples, preferred_element_type=jnp.float32)
        placing = ((tile_goal[chosen][:, None] == target_ids[None, :]) & live_lane[:, None]).astype(
            jnp.float32
        )
        return totals + jnp.einsum(
            "kt,krc->trc", placing, product, precision=lax.Precision.HIGHEST
        )

    start_totals = jnp.zeros((tiles_out, tile_size, col_count), jnp.float32)
    turn_count = (live_total + TBATCH - 1) // TBATCH
    return lax.fori_loop(0, turn_count, one_turn, start_totals)


def shards(echo_data, tile_weights, tile_target, tile_offset, tile_count, grid_map, psf_kernel):
    row_count = echo_data.shape[2]
    half_frames = echo_data.shape[4]
    tile_size = tile_weights.shape[-1]
    slot_count = tile_weights.shape[2]
    voxels = grid_map.shape[1]
    tiles_out = voxels // tile_size
    flat_echo = echo_data.reshape(row_count, 2 * half_frames)
    weights = tile_weights.reshape(slot_count, tile_size, tile_size)
    tile_sums = tile_pass(
        flat_echo,
        weights,
        tile_target.reshape(-1),
        tile_offset.reshape(-1),
        tile_count[0, 0],
        tiles_out,
    )
    arranged = jnp.take(tile_sums.reshape(voxels, 2, half_frames), grid_map[0], axis=0)
    arranged = arranged.reshape(LAT_DEV, voxels // LAT_DEV, 2, half_frames)
    beamformed = lax.psum_scatter(arranged, "chan", scatter_dimension=1, tiled=True).astype(
        jnp.bfloat16
    )
    lat_count = beamformed.shape[0]
    depth_count = beamformed.shape[1]
    cell_count = lat_count * depth_count
    own_frames = beamformed.reshape(cell_count, 2, half_frames)
    all_frames = lax.all_gather(own_frames, "frm", axis=2, tiled=True)
    frames = all_frames.shape[2]
    own_flat = own_frames.reshape(cell_count, 2 * half_frames)
    all_flat = all_frames.reshape(cell_count, 2 * frames)
    gram_block = lax.dot_general(
        own_flat, all_flat, (((0,), (0,)), ((), ())), preferred_element_type=jnp.float32
    )
    gram_real = gram_block[:half_frames, :frames] + gram_block[half_frames:, frames:]
    gram_imag = gram_block[:half_frames, frames:] - gram_block[half_frames:, :frames]
    frame_start = lax.axis_index("frm") * half_frames
    echo_real = all_frames[:, 0, :].astype(jnp.float32)
    echo_imag = all_frames[:, 1, :].astype(jnp.float32)
    energy = jnp.sum(echo_real * echo_real + echo_imag * echo_imag)
    gram_real, gram_imag, trace_value = lax.psum((gram_real, gram_imag, energy), ("vox", "chan"))
    factor = frames / trace_value
    norm_real = factor * gram_real
    norm_imag = factor * gram_imag
    full_real, full_imag = (
        lax.all_gather(norm_real, "frm", axis=0, tiled=True),
        lax.all_gather(norm_imag, "frm", axis=0, tiled=True),
    )
    identity = jnp.eye(frames, dtype=jnp.float32)
    poly_real = POLY_COEFFS[3] * full_real + POLY_COEFFS[2] * identity
    poly_imag = POLY_COEFFS[3] * full_imag
    poly_real, poly_imag = complex_times(poly_real, poly_imag, full_real, full_imag)
    poly_real = poly_real + POLY_COEFFS[1] * identity
    cols_real = lax.dynamic_slice_in_dim(full_real, frame_start, half_frames, 1)
    cols_imag = lax.dynamic_slice_in_dim(full_imag, frame_start, half_frames, 1)
    filter_real, filter_imag = complex_times(poly_real, poly_imag, cols_real, cols_imag)
    filter_real = filter_real + POLY_COEFFS[0] * lax.dynamic_slice_in_dim(
        identity, frame_start, half_frames, 1
    )
    out_real, out_imag = complex_times(echo_real, echo_imag, filter_real, filter_imag)
    envelope = jnp.sqrt(out_real * out_real + out_imag * out_imag + 1e-06)
    envelope = envelope.reshape(lat_count, depth_count, half_frames)
    padded = with_halo(envelope, (("vox", 0), ("chan", 1)), 2)
    psf_image = jnp.zeros_like(envelope)
    for shift_a in range(5):
        for shift_b in range(5):
            psf_image = (
                psf_image
                + psf_kernel[shift_a, shift_b]
                * padded[shift_a : shift_a + lat_count, shift_b : shift_b + depth_count]
            )
    return psf_image


def split(value):
    high = value.astype(jnp.bfloat16)
    return high, (value - high.astype(jnp.float32)).astype(jnp.bfloat16)


def beam_kernel(goal_ref, start_ref, live_ref, weights_ref, echo_ref, map_ref, out_ref, small_ref, operator, high_ref, low_ref):
    blocks, voxels, tile = operator.shape
    operator[...] = jnp.zeros_like(operator)
    lane = lax.broadcasted_iota(jnp.int32, (tile, tile), 1)

    slots = weights_ref.shape[0]
    live = live_ref[0]

    def place(turn, carry):
        ready = []
        for index in range(GROUP):
            slot = turn * GROUP + index
            kept = jnp.minimum(slot, slots - 1)
            first = start_ref[kept]
            block = first // tile
            shift = first - block * tile
            rows = pl.ds(pl.multiple_of(goal_ref[kept] * tile, tile), tile)
            turned = pltpu.roll(weights_ref[kept].astype(jnp.float32), shift, 1)
            limit = jnp.where(slot < live, shift, tile)
            least = jnp.where(slot < live, 0, tile)
            ready.append((block, rows, jnp.where(lane >= limit, turned, 0.0), turned, shift, least))
        for block, rows, high, turned, shift, least in ready:
            operator[block, rows, :] += high
            operator[block + 1, rows, :] += jnp.where((lane < shift) & (lane >= least), turned, 0.0)
        return carry

    lax.fori_loop(0, (live + GROUP - 1) // GROUP, place, 0)
    picks = lax.broadcasted_iota(jnp.int32, (voxels, voxels), 0) == map_ref[...]
    picks = picks.astype(jnp.float32).T.astype(jnp.bfloat16)
    for block in range(blocks - 1):
        high, low = split(operator[block])
        columns = slice(block * tile, (block + 1) * tile)
        for part, target in ((high, high_ref), (low, low_ref)):
            moved = jnp.dot(picks, part, preferred_element_type=jnp.float32)
            target[:, columns] = moved.astype(jnp.bfloat16)
    sums = jnp.dot(high_ref[...], echo_ref[...], preferred_element_type=jnp.float32)
    sums += jnp.dot(low_ref[...], echo_ref[...], preferred_element_type=jnp.float32)
    halves, cells, _ = out_ref.shape
    width = cells // LAT_DEV
    for lat in range(LAT_DEV):
        for half in range(halves):
            source = (lat * halves + half) * width
            chosen = sums[source : source + width]
            out_ref[half, lat * width : (lat + 1) * width, :] = chosen
            small_ref[half, lat * width : (lat + 1) * width, :] = chosen.astype(small_ref.dtype)


def gather_kernel(
    count, part_ref, small_ref, out_ref, arrived, swap_send, swap_recv, own_recv, mate_recv, up_send, down_send, mate_send
):
    vox, chan, frm = lax.axis_index("vox"), lax.axis_index("chan"), lax.axis_index("frm")
    beside, mate = {"chan": 1 - chan}, {"frm": 1 - frm}
    above, below = {"vox": vox + 1}, {"vox": vox - 1}
    can_up, can_down = vox + 1 < count, vox > 0
    pieces = swap_send.shape[0]
    height = part_ref.shape[1] // pieces
    barrier = pltpu.get_barrier_semaphore()

    def greet(target):
        pl.semaphore_signal(barrier, inc=1, device_id=target, device_id_type=MESH)

    greet(beside)
    greet(mate)
    pl.when(can_up)(lambda: greet(above))
    pl.when(can_down)(lambda: greet(below))
    pl.semaphore_wait(barrier, 4 - jnp.where(can_up, 0, 1) - jnp.where(can_down, 0, 1))

    def remote(source, target, sent, received, device):
        return pltpu.make_async_remote_copy(
            src_ref=source, dst_ref=target, send_sem=sent, recv_sem=received, device_id=device, device_id_type=MESH
        )

    def rows(piece):
        return pl.ds(piece * height, height)

    def item(block, piece, sent, device):
        place = out_ref.at[block, frm, :, rows(piece)]
        return remote(place, place, sent, own_recv.at[block, piece], device)

    def to_mate(block, piece, owner=None):
        place = out_ref.at[block, frm if owner is None else owner, :, rows(piece)]
        return remote(place, place, mate_send.at[block, piece], mate_recv.at[block, piece], mate)

    def go_up(block, piece):
        return item(block, piece, up_send.at[block, piece], above)

    def go_down(block, piece):
        return item(block, piece, down_send.at[block, piece], below)

    def swap(piece):
        return remote(
            small_ref.at[:, rows(piece)], arrived.at[:, rows(piece)], swap_send.at[piece], swap_recv.at[piece], beside
        )

    def relay(step, piece):
        @pl.when(vox >= step)
        def _():
            item(vox - step, piece, up_send.at[0, piece], above).wait_recv()
            pl.when(can_up)(lambda: go_up(vox - step, piece).start())
            to_mate(vox - step, piece).start()

        @pl.when(vox + step < count)
        def _():
            item(vox + step, piece, down_send.at[0, piece], below).wait_recv()
            pl.when(can_down)(lambda: go_down(vox + step, piece).start())
            to_mate(vox + step, piece).start()

    for piece in range(pieces):
        swap(piece).start()
    for wave in range(pieces + count - 1):
        if wave < pieces:
            swap(wave).wait_recv()
            mine = part_ref[:, rows(wave)] + arrived[:, rows(wave)].astype(jnp.float32)
            out_ref[vox, frm, :, rows(wave)] = mine.astype(out_ref.dtype)
            pl.when(can_up)(lambda: go_up(vox, wave).start())
            pl.when(can_down)(lambda: go_down(vox, wave).start())
            to_mate(vox, wave).start()
        for step in range(1, count):
            piece = wave - step
            if 0 <= piece < pieces:
                relay(step, piece)

    for piece in range(pieces):
        swap(piece).wait_send()
        for block in range(count):
            to_mate(block, piece).wait_send()
            to_mate(block, piece, 1 - frm).wait_recv()
            pl.when(can_up & (vox >= block))(lambda: go_up(block, piece).wait_send())
            pl.when(can_down & (vox <= block))(lambda: go_down(block, piece).wait_send())


def filter_kernel(count, beams_ref, psf_ref, out_ref, high_ref, low_ref, padded):
    vox, chan, frm = lax.axis_index("vox"), lax.axis_index("chan"), lax.axis_index("frm")
    lat, depth, half = out_ref.shape
    cells = lat * depth
    pair = 2 * half
    total = count * 2 * cells
    left = beams_ref[:, 0].reshape(total, pair)
    right = beams_ref[:, 1].reshape(total, pair)

    def gram(first, second):
        block = lax.dot_general(first, second, (((0,), (0,)), ((), ())), preferred_element_type=jnp.float32)
        real = block[:half, :half] + block[half:, half:]
        imag = block[:half, half:] - block[half:, :half]
        return real, imag

    grams = {(0, 0): gram(left, left), (0, 1): gram(left, right), (1, 1): gram(right, right)}
    grams[1, 0] = (grams[0, 1][0].T, -grams[0, 1][1].T)
    eye = lax.broadcasted_iota(jnp.int32, (half, half), 0) == lax.broadcasted_iota(jnp.int32, (half, half), 1)
    diagonal = jnp.where(eye, grams[0, 0][0] + grams[1, 1][0], 0.0)
    trace = jnp.sum(jnp.sum(diagonal, axis=0, keepdims=True), axis=1, keepdims=True)
    factor = (2 * half) / trace
    for (row, column), (real, imag) in grams.items():
        real_parts, imag_parts = split(factor * real), split(factor * imag)
        for target, real_part, imag_part in zip((high_ref, low_ref), real_parts, imag_parts):
            top, side = row * pair, column * pair
            target[top : top + half, side : side + half] = real_part
            target[top : top + half, side + half : side + pair] = imag_part
            target[top + half : top + pair, side : side + half] = -imag_part
            target[top + half : top + pair, side + half : side + pair] = real_part

    before, after = jnp.maximum(vox - 1, 0), jnp.minimum(vox + 1, count - 1)
    edge = 2 * depth

    def both(block, side, rows):
        return jnp.concatenate([beams_ref[block, 0, side, rows], beams_ref[block, 1, side, rows]], axis=1)

    other = 1 - chan
    near = jnp.concatenate(
        [
            both(before, other, slice(cells - edge, cells)),
            both(vox, other, slice(0, cells)),
            both(after, other, slice(0, edge)),
        ],
        axis=0,
    )
    tall = lat + 4
    slots = -(-2 * tall // 16) * 16
    picked = lax.broadcasted_iota(jnp.int32, (slots, tall * depth), 0)
    source = lax.broadcasted_iota(jnp.int32, (slots, tall * depth), 1)
    wanted = (picked // 2) * depth + picked % 2 + jnp.where(chan == 0, 0, depth - 2)
    picks = ((source == wanted) & (picked < 2 * tall)).astype(jnp.float32).astype(jnp.bfloat16)
    near = jnp.dot(picks, near, preferred_element_type=jnp.float32).astype(jnp.bfloat16)
    beams = jnp.concatenate(
        [
            both(before, chan, slice(cells - edge, cells)),
            both(vox, chan, slice(0, cells)),
            both(after, chan, slice(0, edge)),
            near,
        ],
        axis=0,
    )

    def times(left, right_ref, columns):
        return jnp.dot(left, right_ref[:, columns], preferred_element_type=jnp.float32)

    echo = beams.astype(jnp.float32)
    whole = slice(0, 2 * pair)
    term = POLY_COEFFS[3] * times(beams, high_ref, whole) + POLY_COEFFS[2] * echo
    term = times(term.astype(jnp.bfloat16), high_ref, whole) + POLY_COEFFS[1] * echo
    own = pl.ds(pl.multiple_of(frm * pair, pair), pair)
    echo = jnp.where(frm == 0, echo[:, :pair], echo[:, pair:])
    high, low = split(term)
    term = times(high, high_ref, own) + times(high, low_ref, own) + times(low, high_ref, own) + POLY_COEFFS[0] * echo
    envelope = jnp.sqrt(term[:, :half] * term[:, :half] + term[:, half:] * term[:, half:] + 1e-06)

    padded[...] = jnp.zeros_like(padded)
    has_before, has_after = jnp.where(vox > 0, 1.0, 0.0), jnp.where(vox + 1 < count, 1.0, 0.0)
    right_side, left_side = jnp.where(chan == 0, 1.0, 0.0), jnp.where(chan == 0, 0.0, 1.0)
    for line in range(tall):
        scale = has_before if line < 2 else has_after if line >= lat + 2 else None
        middle = envelope[line * depth : (line + 1) * depth]
        start = tall * depth + 2 * line
        rim = envelope[start : start + 2]
        if scale is not None:
            middle, rim = middle * scale, rim * scale
        padded[line, 8 : 8 + depth, :] = middle
        padded[line, 6:8, :] = rim * left_side
        padded[line, 8 + depth : 10 + depth, :] = rim * right_side
    result = jnp.zeros((lat, depth, half), jnp.float32)
    for shift_b in range(5):
        for shift_a in range(5):
            result += psf_ref[shift_a, shift_b] * padded[shift_a : shift_a + lat, 6 + shift_b : 6 + shift_b + depth]
    out_ref[...] = result


def kernel_shards(count, echo_data, tile_weights, tile_target, tile_offset, tile_count, grid_map, psf_kernel):
    rows, half = echo_data.shape[2], echo_data.shape[4]
    slots, tile = tile_weights.shape[2], tile_weights.shape[4]
    voxels = grid_map.shape[1]
    cells, pair = voxels // 2, 2 * half
    depth = cells // LAT_DEV
    vmem, smem = pl.BlockSpec(memory_space=pltpu.VMEM), pl.BlockSpec(memory_space=pltpu.SMEM)
    parts, small = pl.pallas_call(
        beam_kernel,
        name="beam",
        out_shape=[
            jax.ShapeDtypeStruct((2, cells, pair), jnp.float32),
            jax.ShapeDtypeStruct((2, cells, pair), jnp.bfloat16),
        ],
        in_specs=[smem, smem, smem, vmem, vmem, vmem],
        out_specs=[vmem, vmem],
        scratch_shapes=[
            pltpu.VMEM((rows // tile + 1, voxels, tile), jnp.float32),
            pltpu.VMEM((voxels, rows), jnp.bfloat16),
            pltpu.VMEM((voxels, rows), jnp.bfloat16),
        ],
    )(
        tile_target.reshape(-1),
        tile_offset.reshape(-1),
        tile_count.reshape(-1),
        tile_weights.reshape(slots, tile, tile),
        echo_data.reshape(rows, pair),
        grid_map,
    )
    pieces = PIECES
    each = (count, pieces)
    dma = pltpu.SemaphoreType.DMA
    beams = pl.pallas_call(
        functools.partial(gather_kernel, count),
        name="gather",
        out_shape=jax.ShapeDtypeStruct((count, 2, 2, cells, pair), jnp.bfloat16),
        in_specs=[vmem, vmem],
        out_specs=vmem,
        scratch_shapes=[pltpu.VMEM((2, cells, pair), jnp.bfloat16)] + [dma((pieces,))] * 2 + [dma(each)] * 5,
        compiler_params=pltpu.CompilerParams(collective_id=0, has_side_effects=True),
    )(parts, small)
    return pl.pallas_call(
        functools.partial(filter_kernel, count),
        name="filter",
        out_shape=jax.ShapeDtypeStruct((LAT_DEV, depth, half), jnp.float32),
        in_specs=[vmem, smem],
        out_specs=vmem,
        scratch_shapes=[
            pltpu.VMEM((2 * pair, 2 * pair), jnp.bfloat16),
            pltpu.VMEM((2 * pair, 2 * pair), jnp.bfloat16),
            pltpu.VMEM((LAT_DEV + 4, depth + 16, half), jnp.float32),
        ],
    )(beams, psf_kernel)


def solution(mesh):
    in_specs = (
        P(("groups", "vox"), "chan", None, None, "frm"),
        P("vox", "chan", None, None, None),
        P("vox", "chan", None),
        P("vox", "chan", None),
        P("vox", "chan"),
        P("vox", None),
        P(),
    )
    out_specs = P(("groups", "vox"), "chan", "frm")
    body = shards
    if mesh.shape["chan"] == 2 and mesh.shape["frm"] == 2:
        body = functools.partial(kernel_shards, mesh.shape["vox"])
    return jax.shard_map(body, mesh=mesh, in_specs=in_specs, out_specs=out_specs, check_vma=False)
```

profile of v0, /device:TPU:1, one launch (start us, length us, event | category | flops | bytes accessed | tf_op | source)
XLA Modules:
  0.0 47.5 jit_solution(3805941769838470739)
XLA Ops:
  0.7 2.4 %copy.8 = bf16[128,8,2,256]{3,1,2,0:T(8,128)(2,1)} copy(bf16[128,8,2,256]{3,2,1,0:T(2,128)(2,1)} %bitcast.10) | data formatting | bytes 2097152
  3.1 4.8 %beam.1 = (f32[2,128,512]{2,1,0:T(8,128)}, bf16[2,128,512]{2,1,0:T(8,128)(2,1)}) custom-call(s32[64]{0:T(128)} %bitcast.11, s32[64]{0:T(128)} %bitcast.12, s32[1]{0:T(128)} %bitcast.7.live_ref, bf16[64,128,128]{2,1,0:T(8,128)(2,1)} %bitcast.9, bf16[1024,512]{1,0:T(8,128)(2,1)} %bitcast.8, s32[1,256]{1,0:T(1,128)} %map_ref.1), custom_call_target="tpu_custom_call" | custom-call | tf_op jit(solution)/shard_map/beam/pallas_call | solution.py:386
  7.9 31.1 %gather.1.beams_ref = bf16[4,2,2,128,512]{4,3,2,1,0:T(8,128)(2,1)} custom-call(f32[2,128,512]{2,1,0:T(8,128)} %get-tuple-element.7.part_ref, bf16[2,128,512]{2,1,0:T(8,128)(2,1)} %get-tuple-element.8.small_ref), custom_call_target="tpu_custom_call" | custom-call | tf_op jit(solution)/shard_map/gather/pallas_call | solution.py:411
  39.0 8.5 %filter.1 = f32[8,16,256]{2,1,0:T(8,128)} custom-call(bf16[4,2,2,128,512]{4,3,2,1,0:T(8,128)(2,1)} %gather.1.beams_ref, f32[5,5]{1,0:T(8,128)} %psf_ref.1), custom_call_target="tpu_custom_call" | custom-call | tf_op jit(solution)/shard_map/filter/pallas_call | solution.py:420
where the time goes:
time: 47.6 us; the launch traced here: 47.5 us
  Pallas kernels  44.4 us (93%)
  local copies, waits for them, and re-layouts  2.44 us (5%)
  between operations  0.66 us (1%)
    pallas_call x1, Pallas kernels, kernel_shards(): pl.pallas_call(functools.partial(gather_kernel, count), name='gather', ou...  31.1 us
    pallas_call x1, Pallas kernels, kernel_shards(): pl.pallas_call(functools.partial(filter_kernel, count), name='filter', ou...  8.53 us
    pallas_call x1, Pallas kernels, kernel_shards(): pl.pallas_call(beam_kernel, name='beam', out_shape=[jax.ShapeDtypeStruct(...  4.76 us
    unnamed x1, local copies, waits for them, and re-layouts  2.44 us

commit v1 on v0

--- a/solution.py
+++ b/solution.py
@@ -397,6 +397,7 @@
             pltpu.VMEM((voxels, rows), jnp.bfloat16),
             pltpu.VMEM((voxels, rows), jnp.bfloat16),
         ],
+        compiler_params=pltpu.CompilerParams(vmem_limit_bytes=16 << 20),
     )(
         tile_target.reshape(-1),
         tile_offset.reshape(-1),
@@ -415,7 +416,7 @@
         in_specs=[vmem, vmem],
         out_specs=vmem,
         scratch_shapes=[pltpu.VMEM((2, cells, pair), jnp.bfloat16)] + [dma((pieces,))] * 2 + [dma(each)] * 5,
-        compiler_params=pltpu.CompilerParams(collective_id=0, has_side_effects=True),
+        compiler_params=pltpu.CompilerParams(collective_id=0, has_side_effects=True, vmem_limit_bytes=8 << 20),
     )(parts, small)
     return pl.pallas_call(
         functools.partial(filter_kernel, count),
@@ -428,6 +429,7 @@
             pltpu.VMEM((2 * pair, 2 * pair), jnp.bfloat16),
             pltpu.VMEM((LAT_DEV + 4, depth + 16, half), jnp.float32),
         ],
+        compiler_params=pltpu.CompilerParams(vmem_limit_bytes=24 << 20),
     )(beams, psf_kernel)
 
 

time: 47.6 us -> 41.3 us (0.87)
  Pallas kernels: 44.4 us -> 38.7 us
  local copies, waits for them, and re-layouts: 2.44 us -> 1.47 us
    pallas_call x1, Pallas kernels: 4.76 us -> 2.27 us  [kernel_shards(): pl.pallas_call(beam_kernel, name='beam', out_shape=[jax.ShapeDtypeStruct(...]
    pallas_call x1, Pallas kernels: 31.1 us -> 28.9 us  [kernel_shards(): pl.pallas_call(functools.partial(gather_kernel, count), name='gather', ou...]
    pallas_call x1, Pallas kernels: 8.53 us -> 7.52 us  [kernel_shards(): pl.pallas_call(functools.partial(filter_kernel, count), name='filter', ou...]
    unnamed x1 -> x11, local copies, waits for them, and re-layouts: 2.44 us -> 1.47 us
where the time goes in v1:
time: 41.3 us; the launch traced here: 41.1 us
  Pallas kernels  38.7 us (94%)
  local copies, waits for them, and re-layouts  1.47 us (4%)
  between operations  0.88 us (2%)
    pallas_call x1, Pallas kernels, kernel_shards(): pl.pallas_call(functools.partial(gather_kernel, count), name='gather', ou...  28.9 us
    pallas_call x1, Pallas kernels, kernel_shards(): pl.pallas_call(functools.partial(filter_kernel, count), name='filter', ou...  7.52 us
    pallas_call x1, Pallas kernels, kernel_shards(): pl.pallas_call(beam_kernel, name='beam', out_shape=[jax.ShapeDtypeStruct(...  2.27 us
    unnamed x11, local copies, waits for them, and re-layouts  1.47 us

profile of v1, /device:TPU:1, one launch (start us, length us, event | category | flops | bytes accessed | tf_op | source)
XLA Modules:
  0.0 41.1 jit_solution(16385231433552043396)
XLA Ops:
  0.0 0.0 copy-start.2
  0.0 0.0 copy-start.4
  0.0 0.0 copy-start.3
  0.0 0.0 copy-start
  0.8 1.4 %copy.8 = bf16[128,8,2,256]{3,1,2,0:T(8,128)(2,1)S(1)} copy(bf16[128,8,2,256]{3,2,1,0:T(2,128)(2,1)} %bitcast.12) | data formatting | bytes 2097152
  2.3 0.0 copy-done.2
  2.3 0.0 copy-done.4
  2.3 0.0 copy-done.3
  2.3 0.0 copy-done
  2.3 2.3 %beam.1 = (f32[2,128,512]{2,1,0:T(8,128)S(1)}, bf16[2,128,512]{2,1,0:T(8,128)(2,1)S(1)}) custom-call(s32[64]{0:T(128)S(1)} %bitcast.10, s32[64]{0:T(128)S(1)} %bitcast.11, s32[1]{0:T(128)} %bitcast.7.live_ref, bf16[64,128,128]{2,1,0:T(8,128)(2,1)S(1)} %bitcast.9, bf16[1024,512]{1,0:T(8,128)(2,1)S(1)} %bitcast.8, s32[1,256]{1,0:T(1,128)S(1)} %copy-done.2), custom_call_target="tpu_custom_call" | custom-call | tf_op jit(solution)/shard_map/beam/pallas_call | solution.py:386
  4.6 0.0 copy-start.1
  4.6 28.9 %gather.1.beams_ref = bf16[4,2,2,128,512]{4,3,2,1,0:T(8,128)(2,1)S(1)} custom-call(f32[2,128,512]{2,1,0:T(8,128)S(1)} %get-tuple-element.7.part_ref, bf16[2,128,512]{2,1,0:T(8,128)(2,1)S(1)} %get-tuple-element.8.small_ref), custom_call_target="tpu_custom_call" | custom-call | tf_op jit(solution)/shard_map/gather/pallas_call | solution.py:412
  33.5 0.0 copy-done.1
  33.5 7.5 %filter.1 = f32[8,16,256]{2,1,0:T(8,128)} custom-call(bf16[4,2,2,128,512]{4,3,2,1,0:T(8,128)(2,1)S(1)} %gather.1.beams_ref, f32[5,5]{1,0:T(8,128)S(1)} %copy-done.1), custom_call_target="tpu_custom_call" | custom-call | tf_op jit(solution)/shard_map/filter/pallas_call | solution.py:421
Async XLA Ops:
  0.0 2.3 %copy-start.2 = (s32[1,256]{1,0:T(1,128)S(1)}, s32[1,256]{1,0:T(1,128)}, u32[]{:S(2)}) copy-start(s32[1,256]{1,0:T(1,128)} %map_ref.1) | copy-start | bytes 3076
  0.0 2.3 %copy-start.4 = (s32[1,1,64]{2,1,0:T(1,128)S(1)}, s32[1,1,64]{2,1,0:T(1,128)}, u32[]{:S(2)}) copy-start(s32[1,1,64]{2,1,0:T(1,128)} %param.10) | copy-start | bytes 772
  0.0 2.3 %copy-start.3 = (s32[1,1,64]{2,1,0:T(1,128)S(1)}, s32[1,1,64]{2,1,0:T(1,128)}, u32[]{:S(2)}) copy-start(s32[1,1,64]{2,1,0:T(1,128)} %param.9) | copy-start | bytes 772
  0.0 2.3 %copy-start = (bf16[1,1,64,128,128]{4,3,2,1,0:T(8,128)(2,1)S(1)}, bf16[1,1,64,128,128]{4,3,2,1,0:T(8,128)(2,1)}, u32[]{:S(2)}) copy-start(bf16[1,1,64,128,128]{4,3,2,1,0:T(8,128)(2,1)} %param.8) | copy-start | bytes 6291460
  4.6 28.9 %copy-start.1 = (f32[5,5]{1,0:T(8,128)S(1)}, f32[5,5]{1,0:T(8,128)}, u32[]{:S(2)}) copy-start(f32[5,5]{1,0:T(8,128)} %psf_ref.1) | copy-start | bytes 304

commit v2 on v0

v2 whole, which is shorter than its diff:
```python
import functools

import jax
import jax.numpy as jnp
from jax import lax
from jax.experimental import pallas as pl
from jax.experimental.pallas import tpu as pltpu
from jax.sharding import PartitionSpec as P

MESH = pl.DeviceIdType.MESH
PIECES = 4
HOP = 3
GROUP = 8

TBATCH = 8
LAT_DEV = 8


POLY_COEFFS = (1.0, -0.6, 0.15, -0.03)


def with_halo(shard, sides, width):
    for axis, dim in sides:
        devices, length = (lax.axis_size(axis), shard.shape[dim])
        up = [(i, (i + 1) % devices) for i in range(devices - 1)]
        down = [(j, i) for i, j in up]
        last = lax.slice_in_dim(shard, length - width, length, axis=dim)
        leading = lax.slice_in_dim(shard, 0, width, axis=dim)
        before = lax.ppermute(last, axis, up)
        after = lax.ppermute(leading, axis, down)
        shard = jnp.concatenate([before, shard, after], axis=dim)
    return shard


def complex_times(left_real, left_imag, right_real, right_imag):
    level = lax.Precision.HIGH
    real_part = jnp.dot(
        left_real, right_real, precision=level, preferred_element_type=jnp.float32
    ) - jnp.dot(left_imag, right_imag, precision=level, preferred_element_type=jnp.float32)
    imag_part = jnp.dot(
        left_real, right_imag, precision=level, preferred_element_type=jnp.float32
    ) + jnp.dot(left_imag, right_real, precision=level, preferred_element_type=jnp.float32)
    return (real_part, imag_part)


def tile_pass(flat_echo, weights, tile_goal, tile_start, live_total, tiles_out):
    tile_size = weights.shape[-1]
    col_count = flat_echo.shape[-1]
    slot_count = weights.shape[0]
    lane_ids = jnp.arange(TBATCH, dtype=jnp.int32)
    target_ids = jnp.arange(tiles_out, dtype=jnp.int32)
    zero_index = jnp.zeros((), jnp.int32)

    def cut_rows(offset_id):
        return lax.dynamic_slice(flat_echo, (offset_id, zero_index), (tile_size, col_count))

    def one_turn(turn_index, totals):
        where_at = turn_index * TBATCH + lane_ids
        live_lane = where_at < live_total
        chosen = jnp.minimum(where_at, slot_count - 1)
        picked = weights[chosen]
        samples = jax.vmap(cut_rows)(tile_start[chosen])
        product = jnp.einsum("krs,ksc->krc", picked, samples, preferred_element_type=jnp.float32)
        placing = ((tile_goal[chosen][:, None] == target_ids[None, :]) & live_lane[:, None]).astype(
            jnp.float32
        )
        return totals + jnp.einsum(
            "kt,krc->trc", placing, product, precision=lax.Precision.HIGHEST
        )

    start_totals = jnp.zeros((tiles_out, tile_size, col_count), jnp.float32)
    turn_count = (live_total + TBATCH - 1) // TBATCH
    return lax.fori_loop(0, turn_count, one_turn, start_totals)


def shards(echo_data, tile_weights, tile_target, tile_offset, tile_count, grid_map, psf_kernel):
    row_count = echo_data.shape[2]
    half_frames = echo_data.shape[4]
    tile_size = tile_weights.shape[-1]
    slot_count = tile_weights.shape[2]
    voxels = grid_map.shape[1]
    tiles_out = voxels // tile_size
    flat_echo = echo_data.reshape(row_count, 2 * half_frames)
    weights = tile_weights.reshape(slot_count, tile_size, tile_size)
    tile_sums = tile_pass(
        flat_echo,
        weights,
        tile_target.reshape(-1),
        tile_offset.reshape(-1),
        tile_count[0, 0],
        tiles_out,
    )
    arranged = jnp.take(tile_sums.reshape(voxels, 2, half_frames), grid_map[0], axis=0)
    arranged = arranged.reshape(LAT_DEV, voxels // LAT_DEV, 2, half_frames)
    beamformed = lax.psum_scatter(arranged, "chan", scatter_dimension=1, tiled=True).astype(
        jnp.bfloat16
    )
    lat_count = beamformed.shape[0]
    depth_count = beamformed.shape[1]
    cell_count = lat_count * depth_count
    own_frames = beamformed.reshape(cell_count, 2, half_frames)
    all_frames = lax.all_gather(own_frames, "frm", axis=2, tiled=True)
    frames = all_frames.shape[2]
    own_flat = own_frames.reshape(cell_count, 2 * half_frames)
    all_flat = all_frames.reshape(cell_count, 2 * frames)
    gram_block = lax.dot_general(
        own_flat, all_flat, (((0,), (0,)), ((), ())), preferred_element_type=jnp.float32
    )
    gram_real = gram_block[:half_frames, :frames] + gram_block[half_frames:, frames:]
    gram_imag = gram_block[:half_frames, frames:] - gram_block[half_frames:, :frames]
    frame_start = lax.axis_index("frm") * half_frames
    echo_real = all_frames[:, 0, :].astype(jnp.float32)
    echo_imag = all_frames[:, 1, :].astype(jnp.float32)
    energy = jnp.sum(echo_real * echo_real + echo_imag * echo_imag)
    gram_real, gram_imag, trace_value = lax.psum((gram_real, gram_imag, energy), ("vox", "chan"))
    factor = frames / trace_value
    norm_real = factor * gram_real
    norm_imag = factor * gram_imag
    full_real, full_imag = (
        lax.all_gather(norm_real, "frm", axis=0, tiled=True),
        lax.all_gather(norm_imag, "frm", axis=0, tiled=True),
    )
    identity = jnp.eye(frames, dtype=jnp.float32)
    poly_real = POLY_COEFFS[3] * full_real + POLY_COEFFS[2] * identity
    poly_imag = POLY_COEFFS[3] * full_imag
    poly_real, poly_imag = complex_times(poly_real, poly_imag, full_real, full_imag)
    poly_real = poly_real + POLY_COEFFS[1] * identity
    cols_real = lax.dynamic_slice_in_dim(full_real, frame_start, half_frames, 1)
    cols_imag = lax.dynamic_slice_in_dim(full_imag, frame_start, half_frames, 1)
    filter_real, filter_imag = complex_times(poly_real, poly_imag, cols_real, cols_imag)
    filter_real = filter_real + POLY_COEFFS[0] * lax.dynamic_slice_in_dim(
        identity, frame_start, half_frames, 1
    )
    out_real, out_imag = complex_times(echo_real, echo_imag, filter_real, filter_imag)
    envelope = jnp.sqrt(out_real * out_real + out_imag * out_imag + 1e-06)
    envelope = envelope.reshape(lat_count, depth_count, half_frames)
    padded = with_halo(envelope, (("vox", 0), ("chan", 1)), 2)
    psf_image = jnp.zeros_like(envelope)
    for shift_a in range(5):
        for shift_b in range(5):
            psf_image = (
                psf_image
                + psf_kernel[shift_a, shift_b]
                * padded[shift_a : shift_a + lat_count, shift_b : shift_b + depth_count]
            )
    return psf_image


def split(value):
    high = value.astype(jnp.bfloat16)
    return high, (value - high.astype(jnp.float32)).astype(jnp.bfloat16)


def beam_kernel(goal_ref, start_ref, live_ref, weights_ref, map_ref, out_ref, operator):
    blocks, voxels, tile = operator.shape
    operator[...] = jnp.zeros_like(operator)
    lane = lax.broadcasted_iota(jnp.int32, (tile, tile), 1)

    slots = weights_ref.shape[0]
    live = live_ref[0, 0]

    def place(turn, carry):
        ready = []
        for index in range(GROUP):
            slot = turn * GROUP + index
            kept = jnp.minimum(slot, slots - 1)
            first = start_ref[kept]
            block = first // tile
            shift = first - block * tile
            rows = pl.ds(pl.multiple_of(goal_ref[kept] * tile, tile), tile)
            turned = pltpu.roll(weights_ref[kept].astype(jnp.float32), shift, 1)
            limit = jnp.where(slot < live, shift, tile)
            least = jnp.where(slot < live, 0, tile)
            ready.append((block, rows, jnp.where(lane >= limit, turned, 0.0), turned, shift, least))
        for block, rows, high, turned, shift, least in ready:
            operator[block, rows, :] += high
            operator[block + 1, rows, :] += jnp.where((lane < shift) & (lane >= least), turned, 0.0)
        return carry

    lax.fori_loop(0, (live + GROUP - 1) // GROUP, place, 0)
    picks = lax.broadcasted_iota(jnp.int32, (voxels, voxels), 0) == map_ref[...]
    picks = picks.astype(jnp.float32).T.astype(jnp.bfloat16)
    cells = voxels // 2
    width = cells // LAT_DEV
    for block in range(blocks - 1):
        columns = slice(block * tile, (block + 1) * tile)
        for level, value in enumerate(split(operator[block])):
            moved = jnp.dot(picks, value, preferred_element_type=jnp.float32).astype(jnp.bfloat16)
            for lat in range(LAT_DEV):
                for half in range(2):
                    source = (lat * 2 + half) * width
                    target = level * cells + lat * width
                    out_ref[half, target : target + width, columns] = moved[source : source + width]


def gather_kernel(
    count, operator_ref, echo_ref, psf_ref, rows_ref, gram_ref, near_ref, fine_ref, part, small, arrived, beams,
    swap_send, swap_recv, own_recv, mate_recv, up_send, down_send, mate_send, side_send, side_recv,
):
    vox, chan, frm = lax.axis_index("vox"), lax.axis_index("chan"), lax.axis_index("frm")
    beside, mate = {"chan": 1 - chan}, {"frm": 1 - frm}
    above, below = {"vox": vox + 1}, {"vox": vox - 1}
    can_up, can_down = vox + 1 < count, vox > 0
    at_end = (vox == 0) | (vox == count - 1)
    pieces = PIECES
    units = 2 * pieces
    cells, pair = beams.shape[3], beams.shape[4]
    half = pair // 2
    height = cells // pieces
    depth = cells // LAT_DEV
    barrier = pltpu.get_barrier_semaphore()

    def greet(target):
        pl.semaphore_signal(barrier, inc=1, device_id=target, device_id_type=MESH)

    greet(beside)
    greet(mate)
    pl.when(can_up)(lambda: greet(above))
    pl.when(can_down)(lambda: greet(below))

    def sums(side):
        value = jnp.dot(operator_ref[side], echo_ref[...], preferred_element_type=jnp.float32)
        value = value[:cells] + value[cells:]
        part[side] = value
        small[side] = value.astype(small.dtype)

    def remote(source, target, sent, received, device):
        return pltpu.make_async_remote_copy(
            src_ref=source, dst_ref=target, send_sem=sent, recv_sem=received, device_id=device, device_id_type=MESH
        )

    def rows(unit):
        return pl.ds((unit % pieces) * height, height)

    def side_of(unit):
        return chan if unit < pieces else 1 - chan

    def swap(unit, side):
        return remote(
            small.at[side, rows(unit)], arrived.at[side, rows(unit)], swap_send.at[unit], swap_recv.at[unit], beside
        )

    def item(block, unit, sent, device):
        place = beams.at[block, frm, side_of(unit), rows(unit)]
        return remote(place, place, sent, own_recv.at[block, unit], device)

    def to_mate(block, unit, owner=None):
        place = beams.at[block, frm if owner is None else owner, side_of(unit), rows(unit)]
        return remote(place, place, mate_send.at[block, unit], mate_recv.at[block, unit], mate)

    def go_up(block, unit):
        return item(block, unit, up_send.at[block, unit], above)

    def go_down(block, unit):
        return item(block, unit, down_send.at[block, unit], below)

    def cross(block, unit, side=None):
        place = beams.at[block, frm, chan if side is None else side, rows(unit)]
        return remote(place, place, side_send.at[block, unit], side_recv.at[block, unit], beside)

    def own(unit):
        swap(unit, side_of(unit)).wait_recv()
        mine = part[side_of(unit), rows(unit)] + arrived[side_of(unit), rows(unit)].astype(jnp.float32)
        beams[vox, frm, side_of(unit), rows(unit)] = mine.astype(beams.dtype)
        sends = True if unit < pieces else at_end
        pl.when(can_up & sends)(lambda: go_up(vox, unit).start())
        pl.when(can_down & sends)(lambda: go_down(vox, unit).start())
        to_mate(vox, unit).start()

    def relay(step, unit):
        from_below, from_above = vox >= step, vox + step < count
        low, high = vox - step, vox + step
        if unit >= pieces:
            from_below, from_above = from_below & (low == 0), from_above & (high == count - 1)

        @pl.when(from_below)
        def _():
            item(low, unit, up_send.at[0, unit], above).wait_recv()
            pl.when(can_up)(lambda: go_up(low, unit).start())
            if unit < pieces:
                pl.when(low > 0)(lambda: cross(low, unit).start())
            to_mate(low, unit).start()

        @pl.when(from_above)
        def _():
            item(high, unit, down_send.at[0, unit], below).wait_recv()
            pl.when(can_down)(lambda: go_down(high, unit).start())
            if unit < pieces:
                pl.when(high < count - 1)(lambda: cross(high, unit).start())
            to_mate(high, unit).start()

    def crossed(step, unit):
        low, high = vox - step, vox + step

        @pl.when(low > 0)
        def _():
            cross(low, unit, 1 - chan).wait_recv()
            to_mate(low, pieces + unit).start()

        @pl.when(high < count - 1)
        def _():
            cross(high, unit, 1 - chan).wait_recv()
            to_mate(high, pieces + unit).start()

    def from_mate(step):
        def settle(block):
            for unit in range(units):
                to_mate(block, unit, 1 - frm).wait_recv()

        if step == 0:
            settle(vox)
        else:
            pl.when(vox >= step)(lambda: settle(vox - step))
            pl.when(vox + step < count)(lambda: settle(vox + step))

    def gram(block, index, first=False):
        left, right = ((0, 0), (0, 1), (1, 1))[index]
        value = lax.dot_general(
            beams[block, left].reshape(2 * cells, pair),
            beams[block, right].reshape(2 * cells, pair),
            (((0,), (0,)), ((), ())),
            preferred_element_type=jnp.float32,
        )
        if first:
            gram_ref[index] = value
        else:
            gram_ref[index] += value

    def nth(step):
        return jnp.where(2 * vox < count, (vox + step) % count, (vox + count - step) % count)

    tall = LAT_DEV + 4
    slots = near_ref.shape[1] - tall * depth

    def correlation():
        shape = near_ref.shape
        place = lax.broadcasted_iota(jnp.int32, shape, 0)
        source = lax.broadcasted_iota(jnp.int32, shape, 1)
        inside = source < tall * depth
        extra = source - tall * depth
        line = jnp.where(inside, source // depth, extra // 2)
        column = jnp.where(inside, source % depth, extra % 2 + jnp.where(chan == 0, depth, -2))
        down, across = line - place // depth, column - place % depth + 2
        least, most = jnp.where(vox > 0, 0, 2), jnp.where(vox + 1 < count, tall, tall - 2)
        valid = (line >= least) & (line < most) & (across >= 0) & (across < 5)
        key = jnp.where(valid, down * 5 + across, -1)
        value = jnp.zeros(shape, jnp.float32)
        for shift_a in range(5):
            for shift_b in range(5):
                value = jnp.where(key == shift_a * 5 + shift_b, psf_ref[shift_a, shift_b], value)
        near_ref[...], fine_ref[...] = split(value)

    def collect():
        before, after = jnp.maximum(vox - 1, 0), jnp.minimum(vox + 1, count - 1)
        edge = 2 * depth
        total = rows_ref.shape[0] // 2

        def both(side):
            def lines(block, where):
                parts = [beams[block, owner, side, where] for owner in (0, 1)]
                return jnp.concatenate([parts[0][:, :half], parts[1][:, :half], parts[0][:, half:], parts[1][:, half:]], axis=1)

            return [
                lines(before, slice(cells - edge, cells)),
                lines(vox, slice(0, cells)),
                lines(after, slice(0, edge)),
            ]

        other = jnp.concatenate(both(1 - chan), axis=0)
        picked = lax.broadcasted_iota(jnp.int32, (slots, tall * depth), 0)
        source = lax.broadcasted_iota(jnp.int32, (slots, tall * depth), 1)
        wanted = (picked // 2) * depth + picked % 2 + jnp.where(chan == 0, 0, depth - 2)
        picks = ((source == wanted) & (picked < 2 * tall)).astype(jnp.float32).astype(jnp.bfloat16)
        extra = jnp.dot(picks, other, preferred_element_type=jnp.float32).astype(jnp.bfloat16)
        start = 0
        for value in both(chan) + [extra]:
            size = value.shape[0]
            rows_ref[start : start + size, :] = value[:, :pair]
            rows_ref[total + start : total + start + size, :] = value[:, pair:]
            start += size

    def first_stage(index):
        if index == 0:
            from_mate(0)
        gram(vox, index, True)

    def stage(step):
        from_mate(step)
        if step == 1:
            collect()
        for index in range(3):
            gram(nth(step), index)

    events = [(unit, 0, functools.partial(own, unit)) for unit in range(units)]
    events += [(units + 1 + index, 3, functools.partial(first_stage, index)) for index in range(3)]
    events += [(units - 2, 2, correlation)]
    for step in range(1, count):
        last = step * HOP + units - 1
        events += [(step * HOP + unit, 1, functools.partial(relay, step, unit)) for unit in range(units)]
        if step < count - 1:
            start = units + (step - 1) * pieces + HOP - 1
            last = max(last, start + pieces - 1)
            events += [(start + unit, 2, functools.partial(crossed, step, unit)) for unit in range(pieces)]
        events += [(max(last, units + step * pieces + 1) + 1, 4, functools.partial(stage, step))]

    sums(1 - chan)
    pl.semaphore_wait(barrier, 4 - jnp.where(can_up, 0, 1) - jnp.where(can_down, 0, 1))
    for unit in range(pieces):
        swap(unit, 1 - chan).start()
    sums(chan)
    for unit in range(pieces, units):
        swap(unit, chan).start()
    for _, _, action in sorted(events, key=lambda event: event[:2]):
        action()

    for unit in range(units):
        swap(unit, 1 - chan if unit < pieces else chan).wait_send()
        for block in range(count):
            end = block == 0 or block == count - 1
            to_mate(block, unit).wait_send()
            if unit < pieces or end:
                pl.when(can_up & (vox >= block))(lambda: go_up(block, unit).wait_send())
                pl.when(can_down & (vox <= block))(lambda: go_down(block, unit).wait_send())
            if unit < pieces and not end:
                pl.when(vox != block)(lambda: cross(block, unit).wait_send())


def filter_kernel(rows_ref, gram_ref, near_ref, fine_ref, out_ref, real_ref, imag_ref):
    frm = lax.axis_index("frm")
    lat, depth, half = out_ref.shape
    total = rows_ref.shape[0] // 2

    def parts(index):
        block = gram_ref[index]
        return block[:half, :half] + block[half:, half:], block[:half, half:] - block[half:, :half]

    grams = {(0, 0): parts(0), (0, 1): parts(1), (1, 1): parts(2)}
    grams[1, 0] = (grams[0, 1][0].T, -grams[0, 1][1].T)
    eye = lax.broadcasted_iota(jnp.int32, (half, half), 0) == lax.broadcasted_iota(jnp.int32, (half, half), 1)
    diagonal = []
    for (row, column), (real, imag) in grams.items():
        if row == column:
            diagonal.append(jnp.sum(jnp.where(eye, real, 0.0), axis=0, keepdims=True))
            real = jnp.where(eye, 0.0, real)
        place = (slice(row * half, (row + 1) * half), slice(column * half, (column + 1) * half))
        real_ref[place] = real.astype(jnp.bfloat16)
        imag_ref[place] = imag.astype(jnp.bfloat16)
    trace = jnp.sum(diagonal[0] + diagonal[1], axis=1, keepdims=True)
    factor = (2 * half) / trace
    weight = jnp.concatenate(diagonal, axis=1)

    def mine(value):
        return jnp.where(frm == 0, value[:, :half], value[:, half:])

    def times(value, columns):
        value = value.astype(jnp.bfloat16)
        by_real = jnp.dot(value, real_ref[:, columns], preferred_element_type=jnp.float32)
        by_imag = jnp.dot(value, imag_ref[:, columns], preferred_element_type=jnp.float32)
        return jnp.concatenate([by_real[:total] - by_imag[total:], by_imag[:total] + by_real[total:]], axis=0)

    rows = rows_ref[...]
    echo = rows.astype(jnp.float32)
    every = slice(0, 2 * half)
    once = factor * (times(rows, every) + weight * echo)
    twice = factor * (times(once, every) + weight * once)
    mixed = POLY_COEFFS[2] * once + POLY_COEFFS[3] * twice
    own = pl.ds(pl.multiple_of(frm * half, half), half)
    term = factor * (times(mixed, own) + mine(weight) * mine(mixed))
    term += POLY_COEFFS[0] * mine(echo) + POLY_COEFFS[1] * mine(once)
    real, imag = term[:total], term[total:]
    high, low = split(jnp.sqrt(real * real + imag * imag + 1e-06))
    result = jnp.dot(near_ref[...], high, preferred_element_type=jnp.float32)
    result += jnp.dot(near_ref[...], low, preferred_element_type=jnp.float32)
    result += jnp.dot(fine_ref[...], high, preferred_element_type=jnp.float32)
    out_ref[...] = result.reshape(lat, depth, half)


def kernel_shards(count, echo_data, tile_weights, tile_target, tile_offset, tile_count, grid_map, psf_kernel):
    rows, half = echo_data.shape[2], echo_data.shape[4]
    slots, tile = tile_weights.shape[2], tile_weights.shape[4]
    voxels = grid_map.shape[1]
    cells, pair = voxels // 2, 2 * half
    depth = cells // LAT_DEV
    tall = LAT_DEV + 4
    total = tall * depth + -(-2 * tall // 16) * 16
    vmem, smem = pl.BlockSpec(memory_space=pltpu.VMEM), pl.BlockSpec(memory_space=pltpu.SMEM)
    operator = pl.pallas_call(
        beam_kernel,
        name="beam",
        out_shape=jax.ShapeDtypeStruct((2, voxels, rows), jnp.bfloat16),
        in_specs=[smem, smem, smem, vmem, vmem],
        out_specs=vmem,
        scratch_shapes=[pltpu.VMEM((rows // tile + 1, voxels, tile), jnp.float32)],
        compiler_params=pltpu.CompilerParams(vmem_limit_bytes=8 << 20),
    )(
        tile_target.reshape(-1),
        tile_offset.reshape(-1),
        tile_count,
        tile_weights.reshape(slots, tile, tile),
        grid_map,
    )
    dma = pltpu.SemaphoreType.DMA
    units, each, some = (2 * PIECES,), (count, 2 * PIECES), (count, PIECES)
    gathered = pl.pallas_call(
        functools.partial(gather_kernel, count),
        name="gather",
        out_shape=[
            jax.ShapeDtypeStruct((2 * total, pair), jnp.bfloat16),
            jax.ShapeDtypeStruct((3, pair, pair), jnp.float32),
            jax.ShapeDtypeStruct((cells, total), jnp.bfloat16),
            jax.ShapeDtypeStruct((cells, total), jnp.bfloat16),
        ],
        in_specs=[vmem, vmem, smem],
        out_specs=[vmem] * 4,
        scratch_shapes=[
            pltpu.VMEM((2, cells, pair), jnp.float32),
            pltpu.VMEM((2, cells, pair), jnp.bfloat16),
            pltpu.VMEM((2, cells, pair), jnp.bfloat16),
            pltpu.VMEM((count, 2, 2, cells, pair), jnp.bfloat16),
        ]
        + [dma(units)] * 2
        + [dma(each)] * 5
        + [dma(some)] * 2,
        compiler_params=pltpu.CompilerParams(collective_id=0, has_side_effects=True, vmem_limit_bytes=16 << 20),
    )(operator, echo_data.reshape(rows, pair), psf_kernel)
    return pl.pallas_call(
        filter_kernel,
        name="filter",
        out_shape=jax.ShapeDtypeStruct((LAT_DEV, depth, half), jnp.float32),
        in_specs=[vmem] * 4,
        out_specs=vmem,
        scratch_shapes=[pltpu.VMEM((pair, pair), jnp.bfloat16)] * 2,
        compiler_params=pltpu.CompilerParams(vmem_limit_bytes=16 << 20),
    )(*gathered)


def solution(mesh):
    in_specs = (
        P(("groups", "vox"), "chan", None, None, "frm"),
        P("vox", "chan", None, None, None),
        P("vox", "chan", None),
        P("vox", "chan", None),
        P("vox", "chan"),
        P("vox", None),
        P(),
    )
    out_specs = P(("groups", "vox"), "chan", "frm")
    body = shards
    if mesh.shape["chan"] == 2 and mesh.shape["frm"] == 2:
        body = functools.partial(kernel_shards, mesh.shape["vox"])
    return jax.shard_map(body, mesh=mesh, in_specs=in_specs, out_specs=out_specs, check_vma=False)
```

time: 47.6 us -> 37.6 us (0.79); the launches traced: 47.5 us -> 36.9 us
  Pallas kernels: 44.4 us -> 32.4 us
  local copies, waits for them, and re-layouts: 2.44 us -> 3.81 us
    pallas_call x2, Pallas kernels: 13.3 us -> 5.78 us  [the longest x1 3 us: kernel_shards(): pl.pallas_call(filter_kernel, name='filter', out_shape=jax.ShapeDtypeStru...]
    pallas_call x1, Pallas kernels: 31.1 us -> 26.6 us  [kernel_shards(): pl.pallas_call(functools.partial(gather_kernel, count), name='gather', ou...]
    unnamed x1 -> x13, local copies, waits for them, and re-layouts: 2.44 us -> 3.81 us
where the time goes in v2:
time: 37.6 us; the launch traced here: 36.9 us
  Pallas kernels  32.4 us (86%)
  local copies, waits for them, and re-layouts  3.81 us (10%)
  between operations  0.72 us (2%)
    pallas_call x1, Pallas kernels, kernel_shards(): pl.pallas_call(functools.partial(gather_kernel, count), name='gather', ou...  26.6 us
    unnamed x13, local copies, waits for them, and re-layouts  3.81 us
    pallas_call x1, Pallas kernels, kernel_shards(): pl.pallas_call(filter_kernel, name='filter', out_shape=jax.ShapeDtypeStru...  3 us
    pallas_call x1, Pallas kernels, kernel_shards(): pl.pallas_call(beam_kernel, name='beam', out_shape=jax.ShapeDtypeStruct((...  2.78 us

profile of v2, /device:TPU:1, one launch (start us, length us, event | category | flops | bytes accessed | tf_op | source)
XLA Modules:
  0.0 36.9 jit_solution(4159570062322196909)
XLA Ops:
  0.0 0.0 copy-start.1
  0.7 0.0 copy-start
  0.7 1.6 %copy-done = bf16[1,1,64,128,128]{4,3,2,1,0:T(8,128)(2,1)S(1)} copy-done((bf16[1,1,64,128,128]{4,3,2,1,0:T(8,128)(2,1)S(1)}, bf16[1,1,64,128,128]{4,3,2,1,0:T(8,128)(2,1)}, u32[]{:S(2)}) %copy-start) | copy-done | bytes 2097176
  2.3 0.0 copy-start.2
  2.3 0.7 %copy-done.2 = s32[1,256]{1,0:T(1,128)S(1)} copy-done((s32[1,256]{1,0:T(1,128)S(1)}, s32[1,256]{1,0:T(1,128)}, u32[]{:S(2)}) %copy-start.2) | copy-done | bytes 1048
  2.9 0.0 copy-start.3
  2.9 0.7 %copy-done.3 = s32[1,1,64]{2,1,0:T(1,128)S(1)} copy-done((s32[1,1,64]{2,1,0:T(1,128)S(1)}, s32[1,1,64]{2,1,0:T(1,128)}, u32[]{:S(2)}) %copy-start.3) | copy-done | bytes 280
  3.6 0.0 copy-start.4
  3.6 0.7 %copy-done.4 = s32[1,1,64]{2,1,0:T(1,128)S(1)} copy-done((s32[1,1,64]{2,1,0:T(1,128)S(1)}, s32[1,1,64]{2,1,0:T(1,128)}, u32[]{:S(2)}) %copy-start.4) | copy-done | bytes 280
  4.3 0.0 copy-start.5
  4.3 2.8 %beam.1.operator_ref = bf16[2,256,1024]{2,1,0:T(8,128)(2,1)S(1)} custom-call(s32[64]{0:T(128)S(1)} %bitcast.8, s32[64]{0:T(128)S(1)} %bitcast.9, s32[1,1]{1,0:T(1,128)S(6)} %copy.9.live_ref, bf16[64,128,128]{2,1,0:T(8,128)(2,1)S(1)} %bitcast.7, s32[1,256]{1,0:T(1,128)S(1)} %copy-done.2), custom_call_target="tpu_custom_call" | custom-call | tf_op jit(solution)/shard_map/beam/pallas_call | solution.py:487
  7.0 0.0 copy-done.5
  7.0 0.2 copy.8
  7.3 0.0 copy-done.1
  7.3 26.6 %gather.1 = (bf16[448,512]{1,0:T(8,128)(2,1)S(1)}, f32[3,512,512]{2,1,0:T(8,128)S(1)}, bf16[128,224]{1,0:T(8,128)(2,1)S(1)}, bf16[128,224]{1,0:T(8,128)(2,1)S(1)}) custom-call(bf16[2,256,1024]{2,1,0:T(8,128)(2,1)S(1)} %beam.1.operator_ref, bf16[1024,512]{1,0:T(8,128)(2,1)S(1)} %bitcast.6, f32[5,5]{1,0:T(8,128)S(1)} %copy-done.1), custom_call_target="tpu_custom_call" | custom-call | tf_op jit(solution)/shard_map/gather/pallas_call | solution.py:504
  33.9 3.0 %filter.1 = f32[8,16,256]{2,1,0:T(8,128)} custom-call(bf16[448,512]{1,0:T(8,128)(2,1)S(1)} %get-tuple-element.9.rows_ref, f32[3,512,512]{2,1,0:T(8,128)S(1)} %get-tuple-element.10.gram_ref, bf16[128,224]{1,0:T(8,128)(2,1)S(1)} %get-tuple-element.11.near_ref, bf16[128,224]{1,0:T(8,128)(2,1)S(1)} %get-tuple-element.12.fine_ref), custom_call_target="tpu_custom_call" | custom-call | tf_op jit(solution)/shard_map/filter/pallas_call | solution.py:526
Async XLA Ops:
  0.0 7.3 %copy-start.1 = (f32[5,5]{1,0:T(8,128)S(1)}, f32[5,5]{1,0:T(8,128)}, u32[]{:S(2)}) copy-start(f32[5,5]{1,0:T(8,128)} %psf_ref.1) | copy-start | bytes 304
  0.7 1.6 %copy-start = (bf16[1,1,64,128,128]{4,3,2,1,0:T(8,128)(2,1)S(1)}, bf16[1,1,64,128,128]{4,3,2,1,0:T(8,128)(2,1)}, u32[]{:S(2)}) copy-start(bf16[1,1,64,128,128]{4,3,2,1,0:T(8,128)(2,1)} %param.8) | copy-start | bytes 6291460
  2.3 0.7 %copy-start.2 = (s32[1,256]{1,0:T(1,128)S(1)}, s32[1,256]{1,0:T(1,128)}, u32[]{:S(2)}) copy-start(s32[1,256]{1,0:T(1,128)} %map_ref.1) | copy-start | bytes 3076
  2.9 0.7 %copy-start.3 = (s32[1,1,64]{2,1,0:T(1,128)S(1)}, s32[1,1,64]{2,1,0:T(1,128)}, u32[]{:S(2)}) copy-start(s32[1,1,64]{2,1,0:T(1,128)} %param.9) | copy-start | bytes 772
  3.6 0.7 %copy-start.4 = (s32[1,1,64]{2,1,0:T(1,128)S(1)}, s32[1,1,64]{2,1,0:T(1,128)}, u32[]{:S(2)}) copy-start(s32[1,1,64]{2,1,0:T(1,128)} %param.10) | copy-start | bytes 772
  4.3 2.8 %copy-start.5 = (bf16[1,1,1024,2,256]{4,3,2,1,0:T(2,128)(2,1)S(1)}, bf16[1,1,1024,2,256]{4,3,2,1,0:T(2,128)(2,1)}, u32[]{:S(2)}) copy-start(bf16[1,1,1024,2,256]{4,3,2,1,0:T(2,128)(2,1)} %param.7) | copy-start | bytes 3145732

commit v3 on v2

--- a/solution.py
+++ b/solution.py
@@ -151,23 +151,44 @@
     return high, (value - high.astype(jnp.float32)).astype(jnp.bfloat16)
 
 
-def beam_kernel(goal_ref, start_ref, live_ref, weights_ref, map_ref, out_ref, operator):
+def beam_kernel(
+    goal_hbm, start_hbm, live_hbm, weights_hbm, map_hbm, out_ref, operator, goal_ref, start_ref, live_ref, weights_ref, map_ref, few, many
+):
     blocks, voxels, tile = operator.shape
+    slots = weights_ref.shape[0]
+    turns = slots // GROUP
+    small = [
+        pltpu.make_async_copy(source, target, few.at[index])
+        for index, (source, target) in enumerate(
+            ((live_hbm, live_ref), (start_hbm, start_ref), (goal_hbm, goal_ref), (map_hbm, map_ref))
+        )
+    ]
+
+    def fetch(turn):
+        span = pl.ds(turn * GROUP, GROUP)
+        return pltpu.make_async_copy(weights_hbm.at[span], weights_ref.at[span], many.at[turn])
+
+    for copy in small:
+        copy.start()
+    for turn in range(turns):
+        fetch(turn).start()
     operator[...] = jnp.zeros_like(operator)
     lane = lax.broadcasted_iota(jnp.int32, (tile, tile), 1)
-
-    slots = weights_ref.shape[0]
+    for copy in small:
+        copy.wait()
     live = live_ref[0, 0]
+    used = (live + GROUP - 1) // GROUP
 
     def place(turn, carry):
+        fetch(turn).wait()
         ready = []
         for index in range(GROUP):
-            slot = turn * GROUP + index
-            kept = jnp.minimum(slot, slots - 1)
-            first = start_ref[kept]
+            kept = turn * GROUP + index
+            slot = kept
+            first = start_ref[0, kept]
             block = first // tile
             shift = first - block * tile
-            rows = pl.ds(pl.multiple_of(goal_ref[kept] * tile, tile), tile)
+            rows = pl.ds(pl.multiple_of(goal_ref[0, kept] * tile, tile), tile)
             turned = pltpu.roll(weights_ref[kept].astype(jnp.float32), shift, 1)
             limit = jnp.where(slot < live, shift, tile)
             least = jnp.where(slot < live, 0, tile)
@@ -177,7 +198,7 @@
             operator[block + 1, rows, :] += jnp.where((lane < shift) & (lane >= least), turned, 0.0)
         return carry
 
-    lax.fori_loop(0, (live + GROUP - 1) // GROUP, place, 0)
+    lax.fori_loop(0, used, place, 0)
     picks = lax.broadcasted_iota(jnp.int32, (voxels, voxels), 0) == map_ref[...]
     picks = picks.astype(jnp.float32).T.astype(jnp.bfloat16)
     cells = voxels // 2
@@ -192,18 +213,22 @@
                     target = level * cells + lat * width
                     out_ref[half, target : target + width, columns] = moved[source : source + width]
 
+    def settle(turn, carry):
+        fetch(turn).wait()
+        return carry
+
+    lax.fori_loop(used, turns, settle, 0)
+
 
 def gather_kernel(
-    count, operator_ref, echo_ref, psf_ref, rows_ref, gram_ref, near_ref, fine_ref, part, small, arrived, beams,
-    swap_send, swap_recv, own_recv, mate_recv, up_send, down_send, mate_send, side_send, side_recv,
+    count, operator_ref, echo_ref, psf_ref, rows_ref, gram_ref, near_ref, fine_ref, part, arrived, beams,
+    swap_send, swap_recv, own_recv, mate_recv, up_send, down_send, mate_send, side_send, twin_send, side_recv,
 ):
     vox, chan, frm = lax.axis_index("vox"), lax.axis_index("chan"), lax.axis_index("frm")
     beside, mate = {"chan": 1 - chan}, {"frm": 1 - frm}
     above, below = {"vox": vox + 1}, {"vox": vox - 1}
     can_up, can_down = vox + 1 < count, vox > 0
-    at_end = (vox == 0) | (vox == count - 1)
     pieces = PIECES
-    units = 2 * pieces
     cells, pair = beams.shape[3], beams.shape[4]
     half = pair // 2
     height = cells // pieces
@@ -220,9 +245,7 @@
 
     def sums(side):
         value = jnp.dot(operator_ref[side], echo_ref[...], preferred_element_type=jnp.float32)
-        value = value[:cells] + value[cells:]
-        part[side] = value
-        small[side] = value.astype(small.dtype)
+        part[side] = value[:cells] + value[cells:]
 
     def remote(source, target, sent, received, device):
         return pltpu.make_async_remote_copy(
@@ -235,77 +258,87 @@
     def side_of(unit):
         return chan if unit < pieces else 1 - chan
 
-    def swap(unit, side):
-        return remote(
-            small.at[side, rows(unit)], arrived.at[side, rows(unit)], swap_send.at[unit], swap_recv.at[unit], beside
-        )
+    def swap(unit):
+        return remote(part.at[1 - chan, rows(unit)], arrived.at[rows(unit)], swap_send.at[0], swap_recv.at[unit], beside)
 
     def item(block, unit, sent, device):
         place = beams.at[block, frm, side_of(unit), rows(unit)]
         return remote(place, place, sent, own_recv.at[block, unit], device)
 
-    def to_mate(block, unit, owner=None):
-        place = beams.at[block, frm if owner is None else owner, side_of(unit), rows(unit)]
-        return remote(place, place, mate_send.at[block, unit], mate_recv.at[block, unit], mate)
+    def to_mate(block, unit):
+        place = beams.at[block, frm, side_of(unit), rows(unit)]
+        return remote(place, place, mate_send.at[block], mate_recv.at[block, side_of(unit)], mate)
+
+    def mated(block, owner, side):
+        place = beams.at[block, owner, side]
+        return remote(place, place, mate_send.at[block], mate_recv.at[block, side], mate)
 
     def go_up(block, unit):
-        return item(block, unit, up_send.at[block, unit], above)
+        return item(block, unit, up_send.at[block] if unit < pieces else twin_send.at[0], above)
 
     def go_down(block, unit):
-        return item(block, unit, down_send.at[block, unit], below)
+        return item(block, unit, down_send.at[block] if unit < pieces else twin_send.at[1], below)
 
     def cross(block, unit, side=None):
         place = beams.at[block, frm, chan if side is None else side, rows(unit)]
-        return remote(place, place, side_send.at[block, unit], side_recv.at[block, unit], beside)
+        return remote(place, place, side_send.at[block], side_recv.at[block, unit], beside)
 
     def own(unit):
-        swap(unit, side_of(unit)).wait_recv()
-        mine = part[side_of(unit), rows(unit)] + arrived[side_of(unit), rows(unit)].astype(jnp.float32)
-        beams[vox, frm, side_of(unit), rows(unit)] = mine.astype(beams.dtype)
-        sends = True if unit < pieces else at_end
-        pl.when(can_up & sends)(lambda: go_up(vox, unit).start())
-        pl.when(can_down & sends)(lambda: go_down(vox, unit).start())
+        swap(unit).wait_recv()
+        mine = part[chan, rows(unit)] + arrived[rows(unit)]
+        beams[vox, frm, chan, rows(unit)] = mine.astype(beams.dtype)
+        pl.when(can_up)(lambda: go_up(vox, unit).start())
+        pl.when(can_down)(lambda: go_down(vox, unit).start())
+        cross(vox, unit).start()
         to_mate(vox, unit).start()
 
+    def own_other(unit):
+        cross(vox, unit, 1 - chan).wait_recv()
+        pl.when(can_up)(lambda: go_up(vox, pieces + unit).start())
+        pl.when(can_down)(lambda: go_down(vox, pieces + unit).start())
+        to_mate(vox, pieces + unit).start()
+
     def relay(step, unit):
-        from_below, from_above = vox >= step, vox + step < count
         low, high = vox - step, vox + step
-        if unit >= pieces:
-            from_below, from_above = from_below & (low == 0), from_above & (high == count - 1)
-
-        @pl.when(from_below)
+
+        @pl.when(vox >= step)
         def _():
-            item(low, unit, up_send.at[0, unit], above).wait_recv()
+            item(low, unit, up_send.at[0], above).wait_recv()
             pl.when(can_up)(lambda: go_up(low, unit).start())
-            if unit < pieces:
-                pl.when(low > 0)(lambda: cross(low, unit).start())
+            if step > 1:
+                cross(low, unit).start()
             to_mate(low, unit).start()
 
-        @pl.when(from_above)
+        @pl.when(vox + step < count)
         def _():
-            item(high, unit, down_send.at[0, unit], below).wait_recv()
+            item(high, unit, down_send.at[0], below).wait_recv()
             pl.when(can_down)(lambda: go_down(high, unit).start())
-            if unit < pieces:
-                pl.when(high < count - 1)(lambda: cross(high, unit).start())
+            if step > 1:
+                cross(high, unit).start()
             to_mate(high, unit).start()
 
-    def crossed(step, unit):
+    def other(step, unit):
         low, high = vox - step, vox + step
 
-        @pl.when(low > 0)
+        @pl.when(vox >= step)
         def _():
-            cross(low, unit, 1 - chan).wait_recv()
+            if step > 1:
+                cross(low, unit, 1 - chan).wait_recv()
+            else:
+                item(low, pieces + unit, up_send.at[0], above).wait_recv()
             to_mate(low, pieces + unit).start()
 
-        @pl.when(high < count - 1)
+        @pl.when(vox + step < count)
         def _():
-            cross(high, unit, 1 - chan).wait_recv()
+            if step > 1:
+                cross(high, unit, 1 - chan).wait_recv()
+            else:
+                item(high, pieces + unit, down_send.at[0], below).wait_recv()
             to_mate(high, pieces + unit).start()
 
-    def from_mate(step):
+    def from_mate(step, side):
         def settle(block):
-            for unit in range(units):
-                to_mate(block, unit, 1 - frm).wait_recv()
+            mated(block, 1 - frm, side).wait_recv()
 
         if step == 0:
             settle(vox)
@@ -313,13 +346,14 @@
             pl.when(vox >= step)(lambda: settle(vox - step))
             pl.when(vox + step < count)(lambda: settle(vox + step))
 
-    def gram(block, index, first=False):
+    def gram(halves, index, first=False):
         left, right = ((0, 0), (0, 1), (1, 1))[index]
+
+        def take(owner):
+            return jnp.concatenate([beams[block, owner, side] for block, side in halves], axis=0)
+
         value = lax.dot_general(
-            beams[block, left].reshape(2 * cells, pair),
-            beams[block, right].reshape(2 * cells, pair),
-            (((0,), (0,)), ((), ())),
-            preferred_element_type=jnp.float32,
+            take(left), take(right), (((0,), (0,)), ((), ())), preferred_element_type=jnp.float32
         )
         if first:
             gram_ref[index] = value
@@ -345,84 +379,103 @@
         valid = (line >= least) & (line < most) & (across >= 0) & (across < 5)
         key = jnp.where(valid, down * 5 + across, -1)
         value = jnp.zeros(shape, jnp.float32)
+        taps = psf_ref[...]
         for shift_a in range(5):
             for shift_b in range(5):
-                value = jnp.where(key == shift_a * 5 + shift_b, psf_ref[shift_a, shift_b], value)
+                value = jnp.where(key == shift_a * 5 + shift_b, taps[shift_a : shift_a + 1, shift_b : shift_b + 1], value)
         near_ref[...], fine_ref[...] = split(value)
+
+    def place_rows(start, value):
+        total = rows_ref.shape[0] // 2
+        size = value.shape[0]
+        rows_ref[start : start + size, :] = value[:, :pair]
+        rows_ref[total + start : total + start + size, :] = value[:, pair:]
 
     def collect():
         before, after = jnp.maximum(vox - 1, 0), jnp.minimum(vox + 1, count - 1)
         edge = 2 * depth
-        total = rows_ref.shape[0] // 2
 
         def both(side):
             def lines(block, where):
                 parts = [beams[block, owner, side, where] for owner in (0, 1)]
-                return jnp.concatenate([parts[0][:, :half], parts[1][:, :half], parts[0][:, half:], parts[1][:, half:]], axis=1)
-
-            return [
-                lines(before, slice(cells - edge, cells)),
-                lines(vox, slice(0, cells)),
-                lines(after, slice(0, edge)),
-            ]
-
-        other = jnp.concatenate(both(1 - chan), axis=0)
+                return jnp.concatenate(
+                    [parts[0][:, :half], parts[1][:, :half], parts[0][:, half:], parts[1][:, half:]], axis=1
+                )
+
+            return jnp.concatenate(
+                [
+                    lines(before, slice(cells - edge, cells)),
+                    lines(vox, slice(0, cells)),
+                    lines(after, slice(0, edge)),
+                ],
+                axis=0,
+            )
+
         picked = lax.broadcasted_iota(jnp.int32, (slots, tall * depth), 0)
         source = lax.broadcasted_iota(jnp.int32, (slots, tall * depth), 1)
         wanted = (picked // 2) * depth + picked % 2 + jnp.where(chan == 0, 0, depth - 2)
         picks = ((source == wanted) & (picked < 2 * tall)).astype(jnp.float32).astype(jnp.bfloat16)
-        extra = jnp.dot(picks, other, preferred_element_type=jnp.float32).astype(jnp.bfloat16)
-        start = 0
-        for value in both(chan) + [extra]:
-            size = value.shape[0]
-            rows_ref[start : start + size, :] = value[:, :pair]
-            rows_ref[total + start : total + start + size, :] = value[:, pair:]
-            start += size
+        extra = jnp.dot(picks, both(1 - chan), preferred_element_type=jnp.float32).astype(jnp.bfloat16)
+        place_rows(0, both(chan))
+        place_rows(tall * depth, extra)
 
     def first_stage(index):
         if index == 0:
-            from_mate(0)
-        gram(vox, index, True)
-
-    def stage(step):
-        from_mate(step)
-        if step == 1:
+            from_mate(0, chan)
+            from_mate(0, 1 - chan)
+        gram([(vox, 0), (vox, 1)], index, True)
+
+    def stage(members):
+        for step, far in members:
+            from_mate(step, 1 - chan if far else chan)
+        if (1, 1) in members:
             collect()
         for index in range(3):
-            gram(nth(step), index)
-
-    events = [(unit, 0, functools.partial(own, unit)) for unit in range(units)]
-    events += [(units + 1 + index, 3, functools.partial(first_stage, index)) for index in range(3)]
-    events += [(units - 2, 2, correlation)]
-    for step in range(1, count):
-        last = step * HOP + units - 1
-        events += [(step * HOP + unit, 1, functools.partial(relay, step, unit)) for unit in range(units)]
-        if step < count - 1:
-            start = units + (step - 1) * pieces + HOP - 1
-            last = max(last, start + pieces - 1)
-            events += [(start + unit, 2, functools.partial(crossed, step, unit)) for unit in range(pieces)]
-        events += [(max(last, units + step * pieces + 1) + 1, 4, functools.partial(stage, step))]
+            gram([(nth(step), 1 - chan if far else chan) for step, far in members], index)
+
+    def ready(step, far):
+        if far:
+            return 4 * pieces - 1 if step == 1 else 2 * pieces + 3 * step + 2
+        return 2 * (pieces - 1) + HOP * step
+
+    events = [(2 * pieces - 2, 2, correlation)]
+    for unit in range(pieces):
+        events += [(2 * unit, 0, functools.partial(own, unit))]
+        events += [(2 * pieces - 1 + unit, 1, functools.partial(own_other, unit))]
+        for step in range(1, count):
+            events += [(2 * unit + HOP * step, 1, functools.partial(relay, step, unit))]
+            when = 3 * pieces + unit if step == 1 else 2 * unit + HOP * step + 4
+            events += [(when, 1, functools.partial(other, step, unit))]
+    events += [(3 * pieces - 1, 3, functools.partial(first_stage, index)) for index in range(3)]
+    order = [(step, far) for far in (0, 1) for step in range(1, count)]
+    latest = 0
+    for turn in range(count - 1):
+        members = order[2 * turn : 2 * turn + 2]
+        latest = max([latest] + [ready(*member) for member in members]) + 1
+        events += [(latest, 4, functools.partial(stage, members))]
 
     sums(1 - chan)
     pl.semaphore_wait(barrier, 4 - jnp.where(can_up, 0, 1) - jnp.where(can_down, 0, 1))
     for unit in range(pieces):
-        swap(unit, 1 - chan).start()
+        swap(unit).start()
     sums(chan)
-    for unit in range(pieces, units):
-        swap(unit, chan).start()
     for _, _, action in sorted(events, key=lambda event: event[:2]):
         action()
 
-    for unit in range(units):
-        swap(unit, 1 - chan if unit < pieces else chan).wait_send()
-        for block in range(count):
-            end = block == 0 or block == count - 1
-            to_mate(block, unit).wait_send()
-            if unit < pieces or end:
-                pl.when(can_up & (vox >= block))(lambda: go_up(block, unit).wait_send())
-                pl.when(can_down & (vox <= block))(lambda: go_down(block, unit).wait_send())
-            if unit < pieces and not end:
-                pl.when(vox != block)(lambda: cross(block, unit).wait_send())
+    remote(part.at[1 - chan], arrived, swap_send.at[0], swap_recv.at[0], beside).wait_send()
+    twin = beams.at[vox, frm, 1 - chan]
+    pl.when(can_up)(remote(twin, twin, twin_send.at[0], own_recv.at[0, 0], above).wait_send)
+    pl.when(can_down)(remote(twin, twin, twin_send.at[1], own_recv.at[0, 0], below).wait_send)
+    for block in range(count):
+        mated(block, frm, 0).wait_send()
+        mated(block, frm, 1).wait_send()
+        place = beams.at[block, frm, chan]
+        up = remote(place, place, up_send.at[block], own_recv.at[block, 0], above)
+        down = remote(place, place, down_send.at[block], own_recv.at[block, 0], below)
+        side = remote(place, place, side_send.at[block], side_recv.at[block, 0], beside)
+        pl.when(can_up & (vox >= block))(up.wait_send)
+        pl.when(can_down & (vox <= block))(down.wait_send)
+        pl.when((vox != block + 1) & (vox != block - 1))(side.wait_send)
 
 
 def filter_kernel(rows_ref, gram_ref, near_ref, fine_ref, out_ref, real_ref, imag_ref):
@@ -483,24 +536,37 @@
     depth = cells // LAT_DEV
     tall = LAT_DEV + 4
     total = tall * depth + -(-2 * tall // 16) * 16
-    vmem, smem = pl.BlockSpec(memory_space=pltpu.VMEM), pl.BlockSpec(memory_space=pltpu.SMEM)
+    vmem = pl.BlockSpec(memory_space=pltpu.VMEM)
     operator = pl.pallas_call(
         beam_kernel,
         name="beam",
         out_shape=jax.ShapeDtypeStruct((2, voxels, rows), jnp.bfloat16),
-        in_specs=[smem, smem, smem, vmem, vmem],
+        in_specs=[pl.BlockSpec(memory_space=pltpu.HBM)] * 5,
         out_specs=vmem,
-        scratch_shapes=[pltpu.VMEM((rows // tile + 1, voxels, tile), jnp.float32)],
+        scratch_shapes=[
+            pltpu.VMEM((rows // tile + 1, voxels, tile), jnp.float32),
+            pltpu.SMEM((1, slots), jnp.int32),
+            pltpu.SMEM((1, slots), jnp.int32),
+            pltpu.SMEM((1, 1), jnp.int32),
+            pltpu.VMEM((slots, tile, tile), jnp.bfloat16),
+            pltpu.VMEM((1, voxels), jnp.int32),
+            pltpu.SemaphoreType.DMA((4,)),
+            pltpu.SemaphoreType.DMA((slots // GROUP,)),
+        ],
         compiler_params=pltpu.CompilerParams(vmem_limit_bytes=8 << 20),
     )(
-        tile_target.reshape(-1),
-        tile_offset.reshape(-1),
-        tile_count,
-        tile_weights.reshape(slots, tile, tile),
-        grid_map,
+        *[
+            pltpu.with_memory_space_constraint(value, pltpu.HBM) if value.size > 1 else value
+            for value in (
+                tile_target.reshape(1, slots),
+                tile_offset.reshape(1, slots),
+                tile_count,
+                tile_weights.reshape(slots, tile, tile),
+                grid_map,
+            )
+        ]
     )
     dma = pltpu.SemaphoreType.DMA
-    units, each, some = (2 * PIECES,), (count, 2 * PIECES), (count, PIECES)
     gathered = pl.pallas_call(
         functools.partial(gather_kernel, count),
         name="gather",
@@ -510,17 +576,19 @@
             jax.ShapeDtypeStruct((cells, total), jnp.bfloat16),
             jax.ShapeDtypeStruct((cells, total), jnp.bfloat16),
         ],
-        in_specs=[vmem, vmem, smem],
+        in_specs=[vmem] * 3,
         out_specs=[vmem] * 4,
         scratch_shapes=[
             pltpu.VMEM((2, cells, pair), jnp.float32),
-            pltpu.VMEM((2, cells, pair), jnp.bfloat16),
-            pltpu.VMEM((2, cells, pair), jnp.bfloat16),
+            pltpu.VMEM((cells, pair), jnp.float32),
             pltpu.VMEM((count, 2, 2, cells, pair), jnp.bfloat16),
+            dma((1,)),
+            dma((PIECES,)),
+            dma((count, 2 * PIECES)),
+            dma((count, 2)),
         ]
-        + [dma(units)] * 2
-        + [dma(each)] * 5
-        + [dma(some)] * 2,
+        + [dma((count,))] * 4
+        + [dma((2,)), dma((count, PIECES))],
         compiler_params=pltpu.CompilerParams(collective_id=0, has_side_effects=True, vmem_limit_bytes=16 << 20),
     )(operator, echo_data.reshape(rows, pair), psf_kernel)
     return pl.pallas_call(

time: 37.6 us -> 35.6 us (0.947); the launches traced: 36.9 us -> 35.5 us
  local copies, waits for them, and re-layouts: 3.81 us -> 0.24 us
  Pallas kernels: 32.4 us -> 34.5 us
    unnamed x13 -> x5, local copies, waits for them, and re-layouts: 3.81 us -> 0.24 us
    pallas_call x1, Pallas kernels: 26.6 us -> 29 us  [kernel_shards(): pl.pallas_call(functools.partial(gather_kernel, count), name='gather', ou...]
where the time goes in v3:
time: 35.6 us; the launch traced here: 35.5 us
  Pallas kernels  34.5 us (97%)
  between operations  0.78 us (2%)
    pallas_call x1, Pallas kernels, kernel_shards(): pl.pallas_call(functools.partial(gather_kernel, count), name='gather', ou...  29 us
    pallas_call x1, Pallas kernels, kernel_shards(): pl.pallas_call(filter_kernel, name='filter', out_shape=jax.ShapeDtypeStru...  3 us
    pallas_call x1, Pallas kernels, kernel_shards(): pl.pallas_call(beam_kernel, name='beam', out_shape=jax.ShapeDtypeStruct((...  2.48 us

profile of v3, /device:TPU:1, one launch (start us, length us, event | category | flops | bytes accessed | tf_op | source)
XLA Modules:
  0.0 35.5 jit_solution(43573139558102132)
XLA Ops:
  0.0 0.0 copy-start
  0.0 0.0 copy-start.1
  0.7 2.5 %beam.1.operator_ref = bf16[2,256,1024]{2,1,0:T(8,128)(2,1)S(1)} custom-call(s32[1,64]{1,0:T(1,128)} %bitcast.9, s32[1,64]{1,0:T(1,128)} %bitcast.10, s32[1,1]{1,0:T(1,128)S(6)} %copy.9.live_hbm, bf16[64,128,128]{2,1,0:T(8,128)(2,1)} %bitcast.7, s32[1,256]{1,0:T(1,128)} %map_hbm.1), custom_call_target="tpu_custom_call" | custom-call | tf_op jit(solution)/shard_map/beam/pallas_call | solution.py:540
  3.2 0.0 copy-done.1
  3.2 0.2 copy.8
  3.5 0.0 copy-done
  3.5 29.0 %gather.1 = (bf16[448,512]{1,0:T(8,128)(2,1)S(1)}, f32[3,512,512]{2,1,0:T(8,128)S(1)}, bf16[128,224]{1,0:T(8,128)(2,1)S(1)}, bf16[128,224]{1,0:T(8,128)(2,1)S(1)}) custom-call(bf16[2,256,1024]{2,1,0:T(8,128)(2,1)S(1)} %beam.1.operator_ref, bf16[1024,512]{1,0:T(8,128)(2,1)S(1)} %bitcast.6, f32[5,5]{1,0:T(8,128)S(1)} %copy-done), custom_call_target="tpu_custom_call" | custom-call | tf_op jit(solution)/shard_map/gather/pallas_call | solution.py:570
  32.5 3.0 %filter.1 = f32[8,16,256]{2,1,0:T(8,128)} custom-call(bf16[448,512]{1,0:T(8,128)(2,1)S(1)} %get-tuple-element.9.rows_ref, f32[3,512,512]{2,1,0:T(8,128)S(1)} %get-tuple-element.10.gram_ref, bf16[128,224]{1,0:T(8,128)(2,1)S(1)} %get-tuple-element.11.near_ref, bf16[128,224]{1,0:T(8,128)(2,1)S(1)} %get-tuple-element.12.fine_ref), custom_call_target="tpu_custom_call" | custom-call | tf_op jit(solution)/shard_map/filter/pallas_call | solution.py:594
Async XLA Ops:
  0.0 3.5 %copy-start = (f32[5,5]{1,0:T(8,128)S(1)}, f32[5,5]{1,0:T(8,128)}, u32[]{:S(2)}) copy-start(f32[5,5]{1,0:T(8,128)} %psf_ref.1) | copy-start | bytes 304
  0.0 3.2 %copy-start.1 = (bf16[1,1,1024,2,256]{4,3,2,1,0:T(2,128)(2,1)S(1)}, bf16[1,1,1024,2,256]{4,3,2,1,0:T(2,128)(2,1)}, u32[]{:S(2)}) copy-start(bf16[1,1,1024,2,256]{4,3,2,1,0:T(2,128)(2,1)} %param.7) | copy-start | bytes 3145732

commit v4 on v3

--- a/solution.py
+++ b/solution.py
@@ -9,7 +9,12 @@
 
 MESH = pl.DeviceIdType.MESH
 PIECES = 4
-HOP = 3
+HOP = 1
+PACE = 2
+LAG = 5
+TWIN = (7, 1)
+SIDE = (12, 1)
+FIRST = 2
 GROUP = 8
 
 TBATCH = 8
@@ -222,7 +227,7 @@
 
 def gather_kernel(
     count, operator_ref, echo_ref, psf_ref, rows_ref, gram_ref, near_ref, fine_ref, part, arrived, beams,
-    swap_send, swap_recv, own_recv, mate_recv, up_send, down_send, mate_send, side_send, twin_send, side_recv,
+    swap_send, swap_recv, own_recv, mate_recv, up_send, down_send, mate_send, side_send, side_recv,
 ):
     vox, chan, frm = lax.axis_index("vox"), lax.axis_index("chan"), lax.axis_index("frm")
     beside, mate = {"chan": 1 - chan}, {"frm": 1 - frm}
@@ -240,8 +245,9 @@
 
     greet(beside)
     greet(mate)
-    pl.when(can_up)(lambda: greet(above))
-    pl.when(can_down)(lambda: greet(below))
+    for step in range(1, count):
+        pl.when(vox + step < count)(functools.partial(greet, {"vox": vox + step}))
+        pl.when(vox >= step)(functools.partial(greet, {"vox": vox - step}))
 
     def sums(side):
         value = jnp.dot(operator_ref[side], echo_ref[...], preferred_element_type=jnp.float32)
@@ -273,11 +279,14 @@
         place = beams.at[block, owner, side]
         return remote(place, place, mate_send.at[block], mate_recv.at[block, side], mate)
 
-    def go_up(block, unit):
-        return item(block, unit, up_send.at[block] if unit < pieces else twin_send.at[0], above)
-
-    def go_down(block, unit):
-        return item(block, unit, down_send.at[block] if unit < pieces else twin_send.at[1], below)
+    def go_up(step, unit):
+        return item(vox, unit, up_send.at[step] if unit < pieces else up_send.at[0], {"vox": vox + step})
+
+    def go_down(step, unit):
+        return item(vox, unit, down_send.at[step] if unit < pieces else down_send.at[0], {"vox": vox - step})
+
+    twin_up = can_up & ((vox == 0) | (vox + 2 == count))
+    twin_down = can_down & ((vox == count - 1) | (vox == 1))
 
     def cross(block, unit, side=None):
         place = beams.at[block, frm, chan if side is None else side, rows(unit)]
@@ -287,15 +296,16 @@
         swap(unit).wait_recv()
         mine = part[chan, rows(unit)] + arrived[rows(unit)]
         beams[vox, frm, chan, rows(unit)] = mine.astype(beams.dtype)
-        pl.when(can_up)(lambda: go_up(vox, unit).start())
-        pl.when(can_down)(lambda: go_down(vox, unit).start())
+        for step in range(count - 1, 0, -1):
+            pl.when(vox + step < count)(lambda: go_up(step, unit).start())
+            pl.when(vox >= step)(lambda: go_down(step, unit).start())
         cross(vox, unit).start()
         to_mate(vox, unit).start()
 
     def own_other(unit):
         cross(vox, unit, 1 - chan).wait_recv()
-        pl.when(can_up)(lambda: go_up(vox, pieces + unit).start())
-        pl.when(can_down)(lambda: go_down(vox, pieces + unit).start())
+        pl.when(twin_up)(lambda: go_up(1, pieces + unit).start())
+        pl.when(twin_down)(lambda: go_down(1, pieces + unit).start())
         to_mate(vox, pieces + unit).start()
 
     def relay(step, unit):
@@ -304,17 +314,19 @@
         @pl.when(vox >= step)
         def _():
             item(low, unit, up_send.at[0], above).wait_recv()
-            pl.when(can_up)(lambda: go_up(low, unit).start())
             if step > 1:
                 cross(low, unit).start()
+            else:
+                pl.when(~twin_down)(lambda: cross(low, unit).start())
             to_mate(low, unit).start()
 
         @pl.when(vox + step < count)
         def _():
             item(high, unit, down_send.at[0], below).wait_recv()
-            pl.when(can_down)(lambda: go_down(high, unit).start())
             if step > 1:
                 cross(high, unit).start()
+            else:
+                pl.when(~twin_up)(lambda: cross(high, unit).start())
             to_mate(high, unit).start()
 
     def other(step, unit):
@@ -325,7 +337,8 @@
             if step > 1:
                 cross(low, unit, 1 - chan).wait_recv()
             else:
-                item(low, pieces + unit, up_send.at[0], above).wait_recv()
+                pl.when(twin_down)(item(low, pieces + unit, up_send.at[0], above).wait_recv)
+                pl.when(~twin_down)(cross(low, unit, 1 - chan).wait_recv)
             to_mate(low, pieces + unit).start()
 
         @pl.when(vox + step < count)
@@ -333,7 +346,8 @@
             if step > 1:
                 cross(high, unit, 1 - chan).wait_recv()
             else:
-                item(high, pieces + unit, down_send.at[0], below).wait_recv()
+                pl.when(twin_up)(item(high, pieces + unit, down_send.at[0], below).wait_recv)
+                pl.when(~twin_up)(cross(high, unit, 1 - chan).wait_recv)
             to_mate(high, pieces + unit).start()
 
     def from_mate(step, side):
@@ -433,29 +447,34 @@
         for index in range(3):
             gram([(nth(step), 1 - chan if far else chan) for step, far in members], index)
 
+    def wave(step, far, unit):
+        if step == 0:
+            return TWIN[0] + TWIN[1] * unit if far else PACE * unit
+        if far and step == 1:
+            return SIDE[0] + SIDE[1] * unit
+        return PACE * unit + FIRST + HOP * step + (LAG if far else 0)
+
     def ready(step, far):
-        if far:
-            return 4 * pieces - 1 if step == 1 else 2 * pieces + 3 * step + 2
-        return 2 * (pieces - 1) + HOP * step
-
-    events = [(2 * pieces - 2, 2, correlation)]
+        return wave(step, far, pieces - 1)
+
+    events = [(wave(0, 0, pieces - 1), 2, correlation)]
     for unit in range(pieces):
-        events += [(2 * unit, 0, functools.partial(own, unit))]
-        events += [(2 * pieces - 1 + unit, 1, functools.partial(own_other, unit))]
+        events += [(wave(0, 0, unit), 0, functools.partial(own, unit))]
+        events += [(wave(0, 1, unit), 1, functools.partial(own_other, unit))]
         for step in range(1, count):
-            events += [(2 * unit + HOP * step, 1, functools.partial(relay, step, unit))]
-            when = 3 * pieces + unit if step == 1 else 2 * unit + HOP * step + 4
-            events += [(when, 1, functools.partial(other, step, unit))]
-    events += [(3 * pieces - 1, 3, functools.partial(first_stage, index)) for index in range(3)]
+            events += [(wave(step, 0, unit), 1, functools.partial(relay, step, unit))]
+            events += [(wave(step, 1, unit), 1, functools.partial(other, step, unit))]
+    begin = wave(0, 1, pieces - 1) + 1
+    events += [(begin, 3, functools.partial(first_stage, index)) for index in range(3)]
     order = [(step, far) for far in (0, 1) for step in range(1, count)]
-    latest = 0
+    latest = begin
     for turn in range(count - 1):
         members = order[2 * turn : 2 * turn + 2]
         latest = max([latest] + [ready(*member) for member in members]) + 1
         events += [(latest, 4, functools.partial(stage, members))]
 
     sums(1 - chan)
-    pl.semaphore_wait(barrier, 4 - jnp.where(can_up, 0, 1) - jnp.where(can_down, 0, 1))
+    pl.semaphore_wait(barrier, count + 1)
     for unit in range(pieces):
         swap(unit).start()
     sums(chan)
@@ -464,18 +483,20 @@
 
     remote(part.at[1 - chan], arrived, swap_send.at[0], swap_recv.at[0], beside).wait_send()
     twin = beams.at[vox, frm, 1 - chan]
-    pl.when(can_up)(remote(twin, twin, twin_send.at[0], own_recv.at[0, 0], above).wait_send)
-    pl.when(can_down)(remote(twin, twin, twin_send.at[1], own_recv.at[0, 0], below).wait_send)
+    pl.when(twin_up)(remote(twin, twin, up_send.at[0], own_recv.at[0, 0], above).wait_send)
+    pl.when(twin_down)(remote(twin, twin, down_send.at[0], own_recv.at[0, 0], below).wait_send)
+    place = beams.at[vox, frm, chan]
+    for step in range(1, count):
+        up = remote(place, place, up_send.at[step], own_recv.at[0, 0], {"vox": vox + step})
+        down = remote(place, place, down_send.at[step], own_recv.at[0, 0], {"vox": vox - step})
+        pl.when(vox + step < count)(up.wait_send)
+        pl.when(vox >= step)(down.wait_send)
     for block in range(count):
         mated(block, frm, 0).wait_send()
         mated(block, frm, 1).wait_send()
-        place = beams.at[block, frm, chan]
-        up = remote(place, place, up_send.at[block], own_recv.at[block, 0], above)
-        down = remote(place, place, down_send.at[block], own_recv.at[block, 0], below)
         side = remote(place, place, side_send.at[block], side_recv.at[block, 0], beside)
-        pl.when(can_up & (vox >= block))(up.wait_send)
-        pl.when(can_down & (vox <= block))(down.wait_send)
-        pl.when((vox != block + 1) & (vox != block - 1))(side.wait_send)
+        by_twin = (twin_down & (vox == block + 1)) | (twin_up & (vox + 1 == block))
+        pl.when(~by_twin)(side.wait_send)
 
 
 def filter_kernel(rows_ref, gram_ref, near_ref, fine_ref, out_ref, real_ref, imag_ref):
@@ -588,7 +609,7 @@
             dma((count, 2)),
         ]
         + [dma((count,))] * 4
-        + [dma((2,)), dma((count, PIECES))],
+        + [dma((count, PIECES))],
         compiler_params=pltpu.CompilerParams(collective_id=0, has_side_effects=True, vmem_limit_bytes=16 << 20),
     )(operator, echo_data.reshape(rows, pair), psf_kernel)
     return pl.pallas_call(

time: 35.6 us -> 34.3 us (0.963)
  Pallas kernels: 34.5 us -> 33.1 us
    pallas_call x1, Pallas kernels: 29 us -> 27.6 us  [kernel_shards(): pl.pallas_call(functools.partial(gather_kernel, count), name='gather', ou...]
where the time goes in v4:
time: 34.3 us; the launch traced here: 34.1 us
  Pallas kernels  33.1 us (97%)
  between operations  0.78 us (2%)
    pallas_call x1, Pallas kernels, kernel_shards(): pl.pallas_call(functools.partial(gather_kernel, count), name='gather', ou...  27.6 us
    pallas_call x1, Pallas kernels, kernel_shards(): pl.pallas_call(filter_kernel, name='filter', out_shape=jax.ShapeDtypeStru...  3 us
    pallas_call x1, Pallas kernels, kernel_shards(): pl.pallas_call(beam_kernel, name='beam', out_shape=jax.ShapeDtypeStruct((...  2.48 us

profile of v4, /device:TPU:1, one launch (start us, length us, event | category | flops | bytes accessed | tf_op | source)
XLA Modules:
  0.0 34.1 jit_solution(12981664329551675908)
XLA Ops:
  0.0 0.0 copy-start
  0.0 0.0 copy-start.1
  0.7 2.5 %beam.1.operator_ref = bf16[2,256,1024]{2,1,0:T(8,128)(2,1)S(1)} custom-call(s32[1,64]{1,0:T(1,128)} %bitcast.9, s32[1,64]{1,0:T(1,128)} %bitcast.10, s32[1,1]{1,0:T(1,128)S(6)} %copy.9.live_hbm, bf16[64,128,128]{2,1,0:T(8,128)(2,1)} %bitcast.7, s32[1,256]{1,0:T(1,128)} %map_hbm.1), custom_call_target="tpu_custom_call" | custom-call | tf_op jit(solution)/shard_map/beam/pallas_call | solution.py:561
  3.2 0.0 copy-done.1
  3.2 0.2 copy.8
  3.5 0.0 copy-done
  3.5 27.6 %gather.1 = (bf16[448,512]{1,0:T(8,128)(2,1)S(1)}, f32[3,512,512]{2,1,0:T(8,128)S(1)}, bf16[128,224]{1,0:T(8,128)(2,1)S(1)}, bf16[128,224]{1,0:T(8,128)(2,1)S(1)}) custom-call(bf16[2,256,1024]{2,1,0:T(8,128)(2,1)S(1)} %beam.1.operator_ref, bf16[1024,512]{1,0:T(8,128)(2,1)S(1)} %bitcast.6, f32[5,5]{1,0:T(8,128)S(1)} %copy-done), custom_call_target="tpu_custom_call" | custom-call | tf_op jit(solution)/shard_map/gather/pallas_call | solution.py:591
  31.1 3.0 %filter.1 = f32[8,16,256]{2,1,0:T(8,128)} custom-call(bf16[448,512]{1,0:T(8,128)(2,1)S(1)} %get-tuple-element.9.rows_ref, f32[3,512,512]{2,1,0:T(8,128)S(1)} %get-tuple-element.10.gram_ref, bf16[128,224]{1,0:T(8,128)(2,1)S(1)} %get-tuple-element.11.near_ref, bf16[128,224]{1,0:T(8,128)(2,1)S(1)} %get-tuple-element.12.fine_ref), custom_call_target="tpu_custom_call" | custom-call | tf_op jit(solution)/shard_map/filter/pallas_call | solution.py:615
Async XLA Ops:
  0.0 3.5 %copy-start = (f32[5,5]{1,0:T(8,128)S(1)}, f32[5,5]{1,0:T(8,128)}, u32[]{:S(2)}) copy-start(f32[5,5]{1,0:T(8,128)} %psf_ref.1) | copy-start | bytes 304
  0.0 3.2 %copy-start.1 = (bf16[1,1,1024,2,256]{4,3,2,1,0:T(2,128)(2,1)S(1)}, bf16[1,1,1024,2,256]{4,3,2,1,0:T(2,128)(2,1)}, u32[]{:S(2)}) copy-start(bf16[1,1,1024,2,256]{4,3,2,1,0:T(2,128)(2,1)} %param.7) | copy-start | bytes 3145732

commit v5 on v4

--- a/solution.py
+++ b/solution.py
@@ -13,8 +13,8 @@
 PACE = 2
 LAG = 5
 TWIN = (7, 1)
-SIDE = (12, 1)
-FIRST = 2
+SIDE = (13.1, 1)
+FIRST = 3
 GROUP = 8
 
 TBATCH = 8
@@ -210,13 +210,15 @@
     width = cells // LAT_DEV
     for block in range(blocks - 1):
         columns = slice(block * tile, (block + 1) * tile)
-        for level, value in enumerate(split(operator[block])):
-            moved = jnp.dot(picks, value, preferred_element_type=jnp.float32).astype(jnp.bfloat16)
-            for lat in range(LAT_DEV):
-                for half in range(2):
-                    source = (lat * 2 + half) * width
+        both = jnp.concatenate(split(operator[block]), axis=1)
+        moved = jnp.dot(picks, both, preferred_element_type=jnp.float32).astype(jnp.bfloat16)
+        for lat in range(LAT_DEV):
+            for half in range(2):
+                source = (lat * 2 + half) * width
+                for level in range(2):
                     target = level * cells + lat * width
-                    out_ref[half, target : target + width, columns] = moved[source : source + width]
+                    side = slice(level * tile, (level + 1) * tile)
+                    out_ref[half, target : target + width, columns] = moved[source : source + width, side]
 
     def settle(turn, carry):
         fetch(turn).wait()

time: 34.3 us -> 32.6 us (0.950)
  Pallas kernels: 33.1 us -> 31.3 us
    pallas_call x1, Pallas kernels: 27.6 us -> 25 us  [kernel_shards(): pl.pallas_call(functools.partial(gather_kernel, count), name='gather', ou...]
    pallas_call x1, Pallas kernels: 2.48 us -> 3.25 us  [kernel_shards(): pl.pallas_call(beam_kernel, name='beam', out_shape=jax.ShapeDtypeStruct((...]
where the time goes in v5:
time: 32.6 us; the launch traced here: 32.3 us
  Pallas kernels  31.3 us (96%)
  between operations  0.78 us (2%)
    pallas_call x1, Pallas kernels, kernel_shards(): pl.pallas_call(functools.partial(gather_kernel, count), name='gather', ou...  25 us
    pallas_call x1, Pallas kernels, kernel_shards(): pl.pallas_call(beam_kernel, name='beam', out_shape=jax.ShapeDtypeStruct((...  3.25 us
    pallas_call x1, Pallas kernels, kernel_shards(): pl.pallas_call(filter_kernel, name='filter', out_shape=jax.ShapeDtypeStru...  3 us

profile of v5, /device:TPU:1, one launch (start us, length us, event | category | flops | bytes accessed | tf_op | source)
XLA Modules:
  0.0 32.3 jit_solution(140228073596120649)
XLA Ops:
  0.0 0.0 copy-start
  0.0 0.0 copy-start.1
  0.7 3.3 %beam.1.operator_ref = bf16[2,256,1024]{2,1,0:T(8,128)(2,1)S(1)} custom-call(s32[1,64]{1,0:T(1,128)} %bitcast.9, s32[1,64]{1,0:T(1,128)} %bitcast.10, s32[1,1]{1,0:T(1,128)S(6)} %copy.9.live_hbm, bf16[64,128,128]{2,1,0:T(8,128)(2,1)} %bitcast.7, s32[1,256]{1,0:T(1,128)} %map_hbm.1), custom_call_target="tpu_custom_call" | custom-call | tf_op jit(solution)/shard_map/beam/pallas_call | solution.py:563
  4.0 0.0 copy-done.1
  4.0 0.2 copy.8
  4.3 0.0 copy-done
  4.3 25.0 %gather.1 = (bf16[448,512]{1,0:T(8,128)(2,1)S(1)}, f32[3,512,512]{2,1,0:T(8,128)S(1)}, bf16[128,224]{1,0:T(8,128)(2,1)S(1)}, bf16[128,224]{1,0:T(8,128)(2,1)S(1)}) custom-call(bf16[2,256,1024]{2,1,0:T(8,128)(2,1)S(1)} %beam.1.operator_ref, bf16[1024,512]{1,0:T(8,128)(2,1)S(1)} %bitcast.6, f32[5,5]{1,0:T(8,128)S(1)} %copy-done), custom_call_target="tpu_custom_call" | custom-call | tf_op jit(solution)/shard_map/gather/pallas_call | solution.py:593
  29.3 3.0 %filter.1 = f32[8,16,256]{2,1,0:T(8,128)} custom-call(bf16[448,512]{1,0:T(8,128)(2,1)S(1)} %get-tuple-element.9.rows_ref, f32[3,512,512]{2,1,0:T(8,128)S(1)} %get-tuple-element.10.gram_ref, bf16[128,224]{1,0:T(8,128)(2,1)S(1)} %get-tuple-element.11.near_ref, bf16[128,224]{1,0:T(8,128)(2,1)S(1)} %get-tuple-element.12.fine_ref), custom_call_target="tpu_custom_call" | custom-call | tf_op jit(solution)/shard_map/filter/pallas_call | solution.py:617
Async XLA Ops:
  0.0 4.3 %copy-start = (f32[5,5]{1,0:T(8,128)S(1)}, f32[5,5]{1,0:T(8,128)}, u32[]{:S(2)}) copy-start(f32[5,5]{1,0:T(8,128)} %psf_ref.1) | copy-start | bytes 304
  0.0 4.0 %copy-start.1 = (bf16[1,1,1024,2,256]{4,3,2,1,0:T(2,128)(2,1)S(1)}, bf16[1,1,1024,2,256]{4,3,2,1,0:T(2,128)(2,1)}, u32[]{:S(2)}) copy-start(bf16[1,1,1024,2,256]{4,3,2,1,0:T(2,128)(2,1)} %param.7) | copy-start | bytes 3145732

commit v6 on v5

--- a/solution.py
+++ b/solution.py
@@ -15,7 +15,7 @@
 TWIN = (7, 1)
 SIDE = (13.1, 1)
 FIRST = 3
-GROUP = 8
+GROUP = 16
 
 TBATCH = 8
 LAT_DEV = 8

time: 32.6 us -> 32.2 us (0.988)
    pallas_call x1, Pallas kernels: 3.25 us -> 2.89 us  [kernel_shards(): pl.pallas_call(beam_kernel, name='beam', out_shape=jax.ShapeDtypeStruct((...]
where the time goes in v6:
time: 32.2 us
  Pallas kernels  31.1 us (97%)
  between operations  0.78 us (2%)
    pallas_call x1, Pallas kernels, kernel_shards(): pl.pallas_call(functools.partial(gather_kernel, count), name='gather', ou...  25.2 us
    pallas_call x1, Pallas kernels, kernel_shards(): pl.pallas_call(filter_kernel, name='filter', out_shape=jax.ShapeDtypeStru...  3 us
    pallas_call x1, Pallas kernels, kernel_shards(): pl.pallas_call(beam_kernel, name='beam', out_shape=jax.ShapeDtypeStruct((...  2.89 us

profile of v6, /device:TPU:1, one launch (start us, length us, event | category | flops | bytes accessed | tf_op | source)
XLA Modules:
  0.0 32.2 jit_solution(3026107793340296199)
XLA Ops:
  0.0 0.0 copy-start
  0.0 0.0 copy-start.1
  0.7 2.9 %beam.1.operator_ref = bf16[2,256,1024]{2,1,0:T(8,128)(2,1)S(1)} custom-call(s32[1,64]{1,0:T(1,128)} %bitcast.9, s32[1,64]{1,0:T(1,128)} %bitcast.10, s32[1,1]{1,0:T(1,128)S(6)} %copy.9.live_hbm, bf16[64,128,128]{2,1,0:T(8,128)(2,1)} %bitcast.7, s32[1,256]{1,0:T(1,128)} %map_hbm.1), custom_call_target="tpu_custom_call" | custom-call | tf_op jit(solution)/shard_map/beam/pallas_call | solution.py:563
  3.6 0.0 copy-done.1
  3.7 0.2 copy.8
  3.9 0.0 copy-done
  3.9 25.2 %gather.1 = (bf16[448,512]{1,0:T(8,128)(2,1)S(1)}, f32[3,512,512]{2,1,0:T(8,128)S(1)}, bf16[128,224]{1,0:T(8,128)(2,1)S(1)}, bf16[128,224]{1,0:T(8,128)(2,1)S(1)}) custom-call(bf16[2,256,1024]{2,1,0:T(8,128)(2,1)S(1)} %beam.1.operator_ref, bf16[1024,512]{1,0:T(8,128)(2,1)S(1)} %bitcast.6, f32[5,5]{1,0:T(8,128)S(1)} %copy-done), custom_call_target="tpu_custom_call" | custom-call | tf_op jit(solution)/shard_map/gather/pallas_call | solution.py:593
  29.2 3.0 %filter.1 = f32[8,16,256]{2,1,0:T(8,128)} custom-call(bf16[448,512]{1,0:T(8,128)(2,1)S(1)} %get-tuple-element.9.rows_ref, f32[3,512,512]{2,1,0:T(8,128)S(1)} %get-tuple-element.10.gram_ref, bf16[128,224]{1,0:T(8,128)(2,1)S(1)} %get-tuple-element.11.near_ref, bf16[128,224]{1,0:T(8,128)(2,1)S(1)} %get-tuple-element.12.fine_ref), custom_call_target="tpu_custom_call" | custom-call | tf_op jit(solution)/shard_map/filter/pallas_call | solution.py:617
Async XLA Ops:
  0.0 3.9 %copy-start = (f32[5,5]{1,0:T(8,128)S(1)}, f32[5,5]{1,0:T(8,128)}, u32[]{:S(2)}) copy-start(f32[5,5]{1,0:T(8,128)} %psf_ref.1) | copy-start | bytes 304
  0.0 3.6 %copy-start.1 = (bf16[1,1,1024,2,256]{4,3,2,1,0:T(2,128)(2,1)S(1)}, bf16[1,1,1024,2,256]{4,3,2,1,0:T(2,128)(2,1)}, u32[]{:S(2)}) copy-start(bf16[1,1,1024,2,256]{4,3,2,1,0:T(2,128)(2,1)} %param.7) | copy-start | bytes 3145732

commit v7 on v6

--- a/solution.py
+++ b/solution.py
@@ -15,7 +15,7 @@
 TWIN = (7, 1)
 SIDE = (13.1, 1)
 FIRST = 3
-GROUP = 16
+GROUP = 32
 
 TBATCH = 8
 LAT_DEV = 8

time: 32.2 us -> 32.2 us (level)
    pallas_call x1, Pallas kernels: 2.89 us -> 2.29 us  [kernel_shards(): pl.pallas_call(beam_kernel, name='beam', out_shape=jax.ShapeDtypeStruct((...]
    pallas_call x1, Pallas kernels: 25.2 us -> 25.8 us  [kernel_shards(): pl.pallas_call(functools.partial(gather_kernel, count), name='gather', ou...]
where the time goes in v7:
time: 32.2 us; the launch traced here: 32.1 us
  Pallas kernels  31.1 us (97%)
  between operations  0.78 us (2%)
    pallas_call x1, Pallas kernels, kernel_shards(): pl.pallas_call(functools.partial(gather_kernel, count), name='gather', ou...  25.8 us
    pallas_call x1, Pallas kernels, kernel_shards(): pl.pallas_call(filter_kernel, name='filter', out_shape=jax.ShapeDtypeStru...  3 us
    pallas_call x1, Pallas kernels, kernel_shards(): pl.pallas_call(beam_kernel, name='beam', out_shape=jax.ShapeDtypeStruct((...  2.29 us

profile of v7, /device:TPU:1, one launch (start us, length us, event | category | flops | bytes accessed | tf_op | source)
XLA Modules:
  0.0 32.1 jit_solution(16502545116758419168)
XLA Ops:
  0.0 0.0 copy-start
  0.0 0.0 copy-start.1
  0.7 2.3 %beam.1.operator_ref = bf16[2,256,1024]{2,1,0:T(8,128)(2,1)S(1)} custom-call(s32[1,64]{1,0:T(1,128)} %bitcast.9, s32[1,64]{1,0:T(1,128)} %bitcast.10, s32[1,1]{1,0:T(1,128)S(6)} %copy.9.live_hbm, bf16[64,128,128]{2,1,0:T(8,128)(2,1)} %bitcast.7, s32[1,256]{1,0:T(1,128)} %map_hbm.1), custom_call_target="tpu_custom_call" | custom-call | tf_op jit(solution)/shard_map/beam/pallas_call | solution.py:563
  3.0 0.0 copy-done.1
  3.1 0.2 copy.8
  3.3 0.0 copy-done
  3.3 25.8 %gather.1 = (bf16[448,512]{1,0:T(8,128)(2,1)S(1)}, f32[3,512,512]{2,1,0:T(8,128)S(1)}, bf16[128,224]{1,0:T(8,128)(2,1)S(1)}, bf16[128,224]{1,0:T(8,128)(2,1)S(1)}) custom-call(bf16[2,256,1024]{2,1,0:T(8,128)(2,1)S(1)} %beam.1.operator_ref, bf16[1024,512]{1,0:T(8,128)(2,1)S(1)} %bitcast.6, f32[5,5]{1,0:T(8,128)S(1)} %copy-done), custom_call_target="tpu_custom_call" | custom-call | tf_op jit(solution)/shard_map/gather/pallas_call | solution.py:593
  29.1 3.0 %filter.1 = f32[8,16,256]{2,1,0:T(8,128)} custom-call(bf16[448,512]{1,0:T(8,128)(2,1)S(1)} %get-tuple-element.9.rows_ref, f32[3,512,512]{2,1,0:T(8,128)S(1)} %get-tuple-element.10.gram_ref, bf16[128,224]{1,0:T(8,128)(2,1)S(1)} %get-tuple-element.11.near_ref, bf16[128,224]{1,0:T(8,128)(2,1)S(1)} %get-tuple-element.12.fine_ref), custom_call_target="tpu_custom_call" | custom-call | tf_op jit(solution)/shard_map/filter/pallas_call | solution.py:617
Async XLA Ops:
  0.0 3.3 %copy-start = (f32[5,5]{1,0:T(8,128)S(1)}, f32[5,5]{1,0:T(8,128)}, u32[]{:S(2)}) copy-start(f32[5,5]{1,0:T(8,128)} %psf_ref.1) | copy-start | bytes 304
  0.0 3.0 %copy-start.1 = (bf16[1,1,1024,2,256]{4,3,2,1,0:T(2,128)(2,1)S(1)}, bf16[1,1,1024,2,256]{4,3,2,1,0:T(2,128)(2,1)}, u32[]{:S(2)}) copy-start(bf16[1,1,1024,2,256]{4,3,2,1,0:T(2,128)(2,1)} %param.7) | copy-start | bytes 3145732

commit v8 on v7

--- a/solution.py
+++ b/solution.py
@@ -11,7 +11,7 @@
 PIECES = 4
 HOP = 1
 PACE = 2
-LAG = 5
+LAG = 4.5
 TWIN = (7, 1)
 SIDE = (13.1, 1)
 FIRST = 3
@@ -459,7 +459,7 @@
     def ready(step, far):
         return wave(step, far, pieces - 1)
 
-    events = [(wave(0, 0, pieces - 1), 2, correlation)]
+    events = [(-1, 2, correlation)]
     for unit in range(pieces):
         events += [(wave(0, 0, unit), 0, functools.partial(own, unit))]
         events += [(wave(0, 1, unit), 1, functools.partial(own_other, unit))]

time: 32.2 us -> 32.2 us (level)
  no operation moved by 1% of the time
where the time goes in v8:
time: 32.2 us; the launch traced here: 32.1 us
  Pallas kernels  31.1 us (97%)
  between operations  0.78 us (2%)
    pallas_call x1, Pallas kernels, kernel_shards(): pl.pallas_call(functools.partial(gather_kernel, count), name='gather', ou...  25.8 us
    pallas_call x1, Pallas kernels, kernel_shards(): pl.pallas_call(filter_kernel, name='filter', out_shape=jax.ShapeDtypeStru...  3 us
    pallas_call x1, Pallas kernels, kernel_shards(): pl.pallas_call(beam_kernel, name='beam', out_shape=jax.ShapeDtypeStruct((...  2.29 us

profile of v8, /device:TPU:1, one launch (start us, length us, event | category | flops | bytes accessed | tf_op | source)
XLA Modules:
  0.0 32.1 jit_solution(14303318804894461797)
XLA Ops:
  0.0 0.0 copy-start
  0.0 0.0 copy-start.1
  0.7 2.3 %beam.1.operator_ref = bf16[2,256,1024]{2,1,0:T(8,128)(2,1)S(1)} custom-call(s32[1,64]{1,0:T(1,128)} %bitcast.9, s32[1,64]{1,0:T(1,128)} %bitcast.10, s32[1,1]{1,0:T(1,128)S(6)} %copy.9.live_hbm, bf16[64,128,128]{2,1,0:T(8,128)(2,1)} %bitcast.7, s32[1,256]{1,0:T(1,128)} %map_hbm.1), custom_call_target="tpu_custom_call" | custom-call | tf_op jit(solution)/shard_map/beam/pallas_call | solution.py:563
  3.0 0.0 copy-done.1
  3.1 0.2 copy.8
  3.3 0.0 copy-done
  3.3 25.8 %gather.1 = (bf16[448,512]{1,0:T(8,128)(2,1)S(1)}, f32[3,512,512]{2,1,0:T(8,128)S(1)}, bf16[128,224]{1,0:T(8,128)(2,1)S(1)}, bf16[128,224]{1,0:T(8,128)(2,1)S(1)}) custom-call(bf16[2,256,1024]{2,1,0:T(8,128)(2,1)S(1)} %beam.1.operator_ref, bf16[1024,512]{1,0:T(8,128)(2,1)S(1)} %bitcast.6, f32[5,5]{1,0:T(8,128)S(1)} %copy-done), custom_call_target="tpu_custom_call" | custom-call | tf_op jit(solution)/shard_map/gather/pallas_call | solution.py:593
  29.1 3.0 %filter.1 = f32[8,16,256]{2,1,0:T(8,128)} custom-call(bf16[448,512]{1,0:T(8,128)(2,1)S(1)} %get-tuple-element.9.rows_ref, f32[3,512,512]{2,1,0:T(8,128)S(1)} %get-tuple-element.10.gram_ref, bf16[128,224]{1,0:T(8,128)(2,1)S(1)} %get-tuple-element.11.near_ref, bf16[128,224]{1,0:T(8,128)(2,1)S(1)} %get-tuple-element.12.fine_ref), custom_call_target="tpu_custom_call" | custom-call | tf_op jit(solution)/shard_map/filter/pallas_call | solution.py:617
Async XLA Ops:
  0.0 3.3 %copy-start = (f32[5,5]{1,0:T(8,128)S(1)}, f32[5,5]{1,0:T(8,128)}, u32[]{:S(2)}) copy-start(f32[5,5]{1,0:T(8,128)} %psf_ref.1) | copy-start | bytes 304
  0.0 3.0 %copy-start.1 = (bf16[1,1,1024,2,256]{4,3,2,1,0:T(2,128)(2,1)S(1)}, bf16[1,1,1024,2,256]{4,3,2,1,0:T(2,128)(2,1)}, u32[]{:S(2)}) copy-start(bf16[1,1,1024,2,256]{4,3,2,1,0:T(2,128)(2,1)} %param.7) | copy-start | bytes 3145732
